TPU v7x, 256 devices: a whole 4x4x8 slice. The times are simulated.
256 devices in a mesh: clip: 64 (over x, z, core), cap: 4 (over y).
Axes of the slice: x: 4, y: 4, z: 8, core: 2. Of those that a mesh axis runs over, the one named last changes fastest.
Arguments:
- text: bfloat16 [1024, 512], replicated, may hold values from -8 to 8
- patches: bfloat16 [128, 16, 196, 512], P('clip', None, 'cap'), may hold values from -6 to 6
- frame_slots: int32 [128, 16], P('clip'), may hold values from -1 to 1023, as said below
Outputs:
- contrast_loss: float32 [], replicated
- patch_grad: bfloat16 [128, 16, 196, 512], P('clip', None, 'cap')
- text_grad: float32 [1024, 512], P(('clip', 'cap'))
Inputs may be any that keep to these rules, and one draw needn't show every extreme that they name: `frame_slots`: in every clip the valid frames are the first 4 to 16 slots, and on some index of clip every clip has all 16; all clips together have 128 * 8 valid frames. A valid entry is t * 16 + s: the frame goes to index t of clip, slot s; every index of clip receives exactly 16 frames, one in each slot. A frame stays on its own index of clip unless that index holds more than 16 frames; then its frames past the first 16, in clip and frame order, go to other indices. At most 2 frames go from one index of clip to another, a bound that some pair reaches.
All inputs are finite; a program needn't handle non-finite values.
Results may differ from a plain program's by a relative error of at most 0.0065.
Values may be sent and summed in bfloat16 or wider, within the bound.
A program may use at most 64 MiB of HBM per device.

v0:
```python
import jax
import jax.numpy as jnp
from jax import lax
from jax.sharding import Mesh
from jax.sharding import PartitionSpec as P

WORDS = 8
CLIP = ("clip_0", "clip_1", "clip_2")
CLIP_CAP = ("clip_0", "clip_1", "clip_2", "cap")


logit_scale = 32.0
loss_scale = 8192.0
big_value = 1e30


def sent_to_all(value, axis):
    peers = lax.axis_size(axis)
    return lax.all_to_all(
        jnp.broadcast_to(value[None], (peers, *value.shape)), axis, 0, 0, tiled=True
    )


def in_order(blocks, dim):
    dims = list(blocks.shape[1:])
    dims[dim] *= blocks.shape[0]
    return jnp.moveaxis(blocks, 0, dim).reshape(dims)


def whole_of(value, axes, dim):
    far, near = axes
    first = sent_to_all(value, far)
    blocks = jnp.swapaxes(sent_to_all(first, near), 0, 1)
    return in_order(blocks.reshape(-1, *value.shape), dim)


def sent_together(arrays, axis, dim, along):
    widths = [a.shape[along] for a in arrays]
    both = jnp.concatenate(arrays, axis=along)
    filled = whole_of(both, axis, dim)
    return tuple(jnp.split(filled, [sum(widths[:k]) for k in range(1, len(widths))], axis=along))


def cut_along(value, dim, peers):
    dims = value.shape
    blocks = value.reshape(*dims[:dim], peers, dims[dim] // peers, *dims[dim + 1 :])
    return jnp.moveaxis(blocks, dim, 0)


def sum_at_owner(value, axis, dim):
    blocks = cut_along(value, dim, lax.axis_size(axis))
    arrived = lax.all_to_all(blocks, axis, split_axis=0, concat_axis=0, tiled=True)
    return arrived.sum(axis=0)


def sum_in_two_steps(value, axes, dim):
    far, near = axes
    blocks = cut_along(value, dim, lax.axis_size(far))
    nearer = sum_at_owner(blocks, near, dim + 1)
    arrived = lax.all_to_all(nearer, far, split_axis=0, concat_axis=0, tiled=True)
    return arrived.sum(axis=0)


def block_stats(scores, usable):
    maximum = jnp.max(jnp.where(usable, scores, -big_value), axis=2)
    weight = jnp.where(usable, jnp.exp(scores - maximum[..., None]), 0.0)
    return (maximum, jnp.sum(weight, axis=2), jnp.sum(weight * scores, axis=2))


def merge_groups(maxima, totals, numerators, member):
    inside = member[:, :, None]
    merged_max = jnp.max(jnp.where(inside, maxima[None], -big_value), axis=1)
    factor = jnp.where(inside, jnp.exp(maxima[None] - merged_max[:, None]), 0.0)
    merged_sum = jnp.sum(factor * totals[None], axis=1)
    merged_num = jnp.sum(factor * numerators[None], axis=1)
    return (merged_max, merged_sum, merged_num)


def per_device(text, patches, frame_slots):
    clip_devices = lax.axis_size(CLIP)
    cap_devices = lax.axis_size("cap")
    my_rank = lax.axis_index(CLIP)
    local_clips, frame_max, patch_rows, width = patches.shape
    text_rows = text.shape[0]
    clip_total = clip_devices * local_clips
    quarter = text_rows // cap_devices
    factor_scale = width ** (-0.5)
    frame_total = local_clips * frame_max
    flat_frames = patches.reshape(frame_total, patch_rows, width)
    own_flat = flat_frames.reshape(-1, width)
    scores = (
        lax.dot_general(
            text, own_flat, (((1,), (1,)), ((), ())), preferred_element_type=jnp.float32
        )
        * factor_scale
    )
    scores = scores.reshape(text_rows, local_clips, frame_max * patch_rows)
    usable = jnp.repeat(frame_slots >= 0, patch_rows, axis=1)[None]
    maximum, totals, weighted = block_stats(scores, usable)
    got_max, got_sum, got_num = (
        lax.all_to_all(maximum.T, "cap", split_axis=1, concat_axis=0, tiled=True),
        lax.all_to_all(totals.T, "cap", split_axis=1, concat_axis=0, tiled=True),
        lax.all_to_all(weighted.T, "cap", split_axis=1, concat_axis=0, tiled=True),
    )
    member = jnp.tile(jnp.eye(local_clips, dtype=bool), (1, cap_devices))
    merged_max, merged_sum, merged_num = merge_groups(got_max, got_sum, got_num, member)
    pooled = merged_num / merged_sum
    gathered_max, gathered_sum, gathered_pool = sent_together(
        (merged_max[None], merged_sum[None], pooled[None]),
        (("clip_0", "clip_1"), ("clip_2", "cap")),
        0,
        1,
    )

    def arrange(stacked):
        return (
            stacked.reshape(clip_devices, cap_devices, local_clips, quarter)
            .transpose(0, 2, 1, 3)
            .reshape(clip_total, text_rows)
        )

    all_max = arrange(gathered_max)
    all_sum = arrange(gathered_sum)
    all_pool = arrange(gathered_pool)
    similar = jnp.mean(all_pool.reshape(clip_total, clip_total, WORDS), axis=2)
    logits = logit_scale * similar.T
    row_terms = jax.nn.logsumexp(logits, axis=1)
    col_terms = jax.nn.logsumexp(logits, axis=0)
    matched = jnp.diagonal(logits)
    contrast_loss = 0.5 * (jnp.mean(row_terms - matched) + jnp.mean(col_terms - matched))
    identity = jnp.eye(clip_total, dtype=logits.dtype)
    grad_logits = (
        loss_scale
        * 0.5
        / clip_total
        * (jax.nn.softmax(logits, axis=1) + jax.nn.softmax(logits, axis=0) - 2.0 * identity)
    )
    grad_pooled = jnp.repeat(logit_scale / WORDS * grad_logits.T, WORDS, axis=1)
    first_clip = my_rank * local_clips
    max_rows = lax.dynamic_slice_in_dim(all_max, first_clip, local_clips, 0).T[:, :, None]
    sum_rows = lax.dynamic_slice_in_dim(all_sum, first_clip, local_clips, 0).T[:, :, None]
    pool_rows = lax.dynamic_slice_in_dim(all_pool, first_clip, local_clips, 0).T[:, :, None]
    grad_rows = lax.dynamic_slice_in_dim(grad_pooled, first_clip, local_clips, 0).T[:, :, None]
    weights = jnp.where(usable, jnp.exp(scores - max_rows) / sum_rows, 0.0)
    grad_scores = (grad_rows * weights * (1.0 + scores - pool_rows)).astype(jnp.bfloat16)
    grad_flat = grad_scores.reshape(text_rows, frame_total * patch_rows)
    frame_grad = (
        lax.dot_general(
            grad_flat, text, (((0,), (0,)), ((), ())), preferred_element_type=jnp.float32
        )
        * factor_scale
    )
    frame_grad = frame_grad.astype(jnp.bfloat16).reshape(patches.shape)
    text_part = (
        lax.dot_general(
            grad_flat, own_flat, (((1,), (0,)), ((), ())), preferred_element_type=jnp.float32
        )
        * factor_scale
    )
    text_grad = sum_in_two_steps(text_part, (("clip_0", "clip_1"), ("clip_2", "cap")), 0)
    return (contrast_loss, frame_grad, text_grad)


def solution(mesh):
    finer = Mesh(
        mesh.devices.reshape(4, 8, 2, mesh.shape["cap"]), ("clip_0", "clip_1", "clip_2", "cap")
    )
    in_specs = (P(), P(CLIP, None, "cap", None), P(CLIP, None))
    out_specs = (P(), P(CLIP, None, "cap", None), P(CLIP_CAP, None))
    return jax.shard_map(
        per_device, mesh=finer, in_specs=in_specs, out_specs=out_specs, check_vma=False
    )
```

profile of v0, /device:TPU:1, one launch (start us, length us, event | category | flops | bytes accessed | tf_op | source)
XLA Modules:
  0.0 165.1 jit_solution(10197760124510658843)
XLA Ops:
  0.6 0.0 copy-start
  0.6 0.8 broadcast_compare_fusion
  1.4 0.1 broadcast_in_dim.114
  1.5 0.1 broadcast_in_dim.115
  1.6 2.3 %copy.92 = bf16[2,16,49,512]{3,2,1,0:T(8,128)(2,1)S(1)} copy(bf16[2,16,49,512]{3,1,2,0:T(8,128)(2,1)} %param.4) | data formatting | bytes 3211264 | tf_op args[1]
  3.9 1.4 reshape_reshape.12
  5.3 0.0 copy-done
  5.3 3.3 %convolution_multiply_fusion = f32[1024,1568]{0,1:T(8,128)S(1)} fusion(bf16[1024,512]{1,0:T(8,128)(2,1)S(1)} %copy-done, bf16[1568,512]{1,0:T(8,128)(2,1)} %reshape_reshape.12), kind=kOutput, calls=%fused_computation.13 | convolution fusion | flops 1645772800 | bytes 9076736 | tf_op jit(solution)/shard_map/dot_general | solution.py:92
  8.6 0.0 copy-start.1
  8.6 1.7 %select_reduce_fusion = f32[1024,2]{0,1:T(2,128)} fusion(f32[1024,2,784]{0,2,1:T(8,128)S(1)} %bitcast.99, pred[2,784]{1,0:T(4,128)(4,1)S(1)} %broadcast_in_dim.115), kind=kLoop, calls=%fused_computation.12 | loop fusion | flops 3209216 | bytes 6432288 | tf_op jit(solution)/shard_map/reduce_max | solution.py:65
  10.4 1.0 copy-done.1
  11.4 5.0 %all-to-all-start = ((f32[2,4,256]{2,0,1:T(2,128)}), f32[2,4,256]{2,0,1:T(2,128)S(1)}, u32[]{:S(2)}, u32[]{:S(2)}) async-start(f32[2,4,256]{2,0,1:T(2,128)} %bitcast.2), calls=%async_computation | async-start | bytes 16384 | tf_op jit(solution)/shard_map/all_to_all | solution.py:101
  16.4 4.3 %fusion.5 = (f32[1024,2]{0,1:T(2,128)}, f32[1024,2]{0,1:T(2,128)S(1)}) fusion(f32[1024,2,784]{0,2,1:T(8,128)} %bitcast.100, f32[1024,2]{0,1:T(2,128)} %select_reduce_fusion, pred[2,784]{1,0:T(4,128)(4,1)S(1)} %broadcast_in_dim.115), kind=kLoop, calls=%fused_computation.11 | loop fusion | flops 8024064 | bytes 6448672 | tf_op jit(solution)/shard_map/reduce_sum | solution.py:67
  20.7 0.0 all-to-all-done
  20.7 8.2 %all_to_all.68 = f32[2,4,256]{2,0,1:T(2,128)S(1)} all-to-all(f32[2,4,256]{2,0,1:T(2,128)S(1)} %bitcast.113), channel_id=1, replica_groups=mesh['clip_0'=4,'clip_1'=8,'clip_2'=2,'cap'=4] {'cap'}, dimensions={1} | all-to-all | bytes 16384 | tf_op jit(solution)/shard_map/all_to_all | solution.py:103
  28.9 3.2 %all-to-all-start.1 = ((f32[2,4,256]{2,0,1:T(2,128)}), f32[2,4,256]{2,0,1:T(2,128)S(1)}, u32[]{:S(2)}, u32[]{:S(2)}) async-start(f32[2,4,256]{2,0,1:T(2,128)} %bitcast.6), calls=%async_computation.1 | async-start | bytes 16384 | tf_op jit(solution)/shard_map/all_to_all | solution.py:102
  32.1 0.1 tile.13
  32.3 4.0 %all-to-all-done.1 = f32[2,4,256]{2,0,1:T(2,128)S(1)} async-done(((f32[2,4,256]{2,0,1:T(2,128)}), f32[2,4,256]{2,0,1:T(2,128)S(1)}, u32[]{:S(2)}, u32[]{:S(2)}) %all-to-all-start.1) | async-done | bytes 8224 | tf_op jit(solution)/shard_map/all_to_all | solution.py:102
  36.3 0.1 select_reduce_fusion.1
  36.4 0.1 multiply_reduce_fusion.4
  36.5 0.1 broadcast_in_dim.126
  36.6 20.2 %all_to_all.69 = f32[32,1,6,256]{3,1,2,0:T(1,128)S(1)} all-to-all(f32[32,1,6,256]{3,1,2,0:T(1,128)S(1)} %broadcast_in_dim.126), channel_id=1, replica_groups=mesh['clip_0'=4,'clip_1'=8,'clip_2'=2,'cap'=4] {'clip_0','clip_1'}, dimensions={0} | all-to-all | bytes 393216 | tf_op jit(solution)/shard_map/all_to_all | solution.py:19
  56.8 1.3 broadcast_in_dim.128
  58.2 8.7 %all-to-all-start.4 = ((f32[8,32,1,6,256]{4,1,3,2,0:T(8,128)}), f32[8,32,1,6,256]{4,1,3,2,0:T(8,128)S(1)}, u32[]{:S(2)}, u32[]{:S(2)}) async-start(f32[8,32,1,6,256]{4,1,3,2,0:T(8,128)} %broadcast_in_dim.128), calls=%async_computation.4 | async-start | bytes 3145728 | tf_op jit(solution)/shard_map/all_to_all | solution.py:19
  66.9 0.1 broadcast_in_dim.130
  67.0 20.5 %all-to-all-done.4 = f32[8,32,1,6,256]{4,1,3,2,0:T(8,128)S(1)} async-done(((f32[8,32,1,6,256]{4,1,3,2,0:T(8,128)}), f32[8,32,1,6,256]{4,1,3,2,0:T(8,128)S(1)}, u32[]{:S(2)}, u32[]{:S(2)}) %all-to-all-start.4) | async-done | bytes 1572896 | tf_op jit(solution)/shard_map/all_to_all | solution.py:19
  87.5 0.9 copy.117
  88.4 0.2 fusion.7
  88.6 0.4 copy.101
  89.0 0.1 copy.102
  89.2 0.1 copy.110
  89.3 0.4 copy.103
  89.7 0.1 copy.104
  89.8 0.1 copy.111
  89.9 0.4 copy.97
  90.4 0.1 copy.98
  90.5 6.1 %reshape_reshape.14 = f32[128,128,8]{2,1,0:T(8,128)} reshape(f32[64,2,4,256]{3,2,1,0:T(4,128)S(1)} %copy.98) | data formatting | bytes 1048576 | tf_op jit(solution)/shard_map/reshape;reshape | solution.py:125
  96.6 0.1 copy.112
  96.7 5.6 %reduce_sum.124 = f32[128,128]{1,0:T(8,128)S(1)} reduce(f32[128,128,8]{2,1,0:T(8,128)} %reshape_reshape.14, f32[]{:T(128)} %constant.22.clone.1), dimensions={2}, to_apply=%region_6.7 | reduce | flops 114688 | bytes 589828 | tf_op jit(solution)/shard_map/reduce_sum | solution.py:125
  102.3 0.1 multiply_reduce_fusion.1
  102.5 0.2 exponential_reduce_fusion.1
  102.7 0.1 subtract_multiply_fusion
  102.8 0.1 copy.99
  103.0 0.2 dynamic-slice_bitcast_fusion
  103.2 0.2 copy.100
  103.4 0.0 copy-start.3
  103.4 4.1 %fusion.1 = bf16[1024,1568]{0,1:T(8,128)(2,1)S(1)} fusion(f32[1024,1568]{0,1:T(8,128)} %copy-done.1, f32[1024,2]{0,1:T(2,128)S(1)} %get-tuple-element.46, f32[1024,2]{0,1:T(2,128)S(1)} %get-tuple-element.47, f32[1024,2]{0,1:T(2,128)S(1)} %dynamic-slice_bitcast_fusion.3, f32[1024,2]{0,1:T(2,128)S(1)} %copy.100, pred[1568]{0:T(1024)(128)(4,1)S(1)} %broadcast_in_dim.130), kind=kLoop, calls=%fused_computation.3 | loop fusion | flops 12845056 | bytes 9668128 | tf_op jit(solution)/shard_map/convert_element_type | solution.py:145
  107.5 0.0 copy-start.2
  107.5 1.7 %copy-done.2 = bf16[1024,1568]{0,1:T(8,128)(2,1)} copy-done((bf16[1024,1568]{0,1:T(8,128)(2,1)}, bf16[1024,1568]{0,1:T(8,128)(2,1)S(1)}, u32[]{:S(2)}) %copy-start.2) | copy-done | bytes 3211288
  109.2 0.0 copy-done.3
  109.2 3.4 %convolution_multiply_fusion.2 = f32[1024,512]{1,0:T(8,128)} fusion(bf16[1024,1568]{0,1:T(8,128)(2,1)S(1)} %fusion.1, bf16[1568,512]{1,0:T(8,128)(2,1)S(1)} %copy-done.3), kind=kOutput, calls=%fused_computation.17 | convolution fusion | flops 1644691456 | bytes 6914048 | tf_op jit(solution)/shard_map/dot_general | solution.py:155
  112.6 1.9 %reshape_reshape.15 = f32[32,8,4,512]{3,2,1,0:T(4,128)S(1)} reshape(f32[1024,512]{1,0:T(8,128)} %convolution_multiply_fusion.2) | data formatting | bytes 4194304 | tf_op jit(solution)/shard_map/reshape;reshape | solution.py:46
  114.5 1.8 %copy.116 = f32[32,8,4,512]{3,2,0,1:T(4,128)} copy(f32[32,8,4,512]{3,2,1,0:T(4,128)S(1)} %reshape_reshape.15) | data formatting | bytes 4194304 | tf_op jit(solution)/shard_map/reshape;reshape | solution.py:46
  116.3 3.9 %all-to-all-start.5 = ((f32[8,32,4,512]{3,2,1,0:T(4,128)}), f32[8,32,4,512]{3,2,1,0:T(4,128)S(1)}, u32[]{:S(2)}, u32[]{:S(2)}) async-start(f32[8,32,4,512]{3,2,1,0:T(4,128)} %bitcast.101), calls=%async_computation.5 | async-start | bytes 4194304 | tf_op jit(solution)/shard_map/all_to_all | solution.py:52
  120.2 26.2 %all-to-all-done.5 = f32[8,32,4,512]{3,2,1,0:T(4,128)S(1)} async-done(((f32[8,32,4,512]{3,2,1,0:T(4,128)}), f32[8,32,4,512]{3,2,1,0:T(4,128)S(1)}, u32[]{:S(2)}, u32[]{:S(2)}) %all-to-all-start.5) | async-done | bytes 2097184 | tf_op jit(solution)/shard_map/all_to_all | solution.py:52
  146.4 1.2 reduce_sum.131
  147.6 4.2 %all-to-all-start.6 = ((f32[32,4,512]{2,1,0:T(4,128)}), f32[32,4,512]{2,1,0:T(4,128)S(1)}, u32[]{:S(2)}, u32[]{:S(2)}) async-start(f32[32,4,512]{2,1,0:T(4,128)} %reduce_sum.131), calls=%async_computation.6 | async-start | bytes 524288 | tf_op jit(solution)/shard_map/all_to_all | solution.py:60
  151.8 4.9 %fusion.6 = bf16[1568,512]{1,0:T(8,128)(2,1)} fusion(bf16[1024,1568]{0,1:T(8,128)(2,1)} %copy-done.2, bf16[1024,512]{1,0:T(8,128)(2,1)S(1)} %copy-done), kind=kOutput, calls=%fused_computation.15 | convolution fusion | flops 1645772800 | bytes 5865472 | tf_op jit(solution)/shard_map/dot_general | solution.py:148
  156.7 1.7 %reshape.111 = bf16[2,16,49,512]{3,2,1,0:T(8,128)(2,1)S(1)} reshape(bf16[1568,512]{1,0:T(8,128)(2,1)} %fusion.6) | data formatting | bytes 3211264 | tf_op jit(solution)/shard_map/reshape | solution.py:153
  158.4 1.7 %copy.108 = bf16[2,16,49,512]{3,1,2,0:T(8,128)(2,1)} copy(bf16[2,16,49,512]{3,2,1,0:T(8,128)(2,1)S(1)} %reshape.111) | data formatting | bytes 3211264
  160.1 1.3 gather_fusion
  161.4 0.6 subtract_reduce_fusion
  163.3 0.0 all-to-all-done.6
  163.3 0.7 reduce_sum.132
  (13 shorter events, 0.2 us)
Async XLA Ops:
  0.6 4.7 %copy-start = (bf16[1024,512]{1,0:T(8,128)(2,1)S(1)}, bf16[1024,512]{1,0:T(8,128)(2,1)}, u32[]{:S(2)}) copy-start(bf16[1024,512]{1,0:T(8,128)(2,1)} %param.3) | copy-start | bytes 3145732
  8.6 2.7 %copy-start.1 = (f32[1024,1568]{0,1:T(8,128)}, f32[1024,1568]{0,1:T(8,128)S(1)}, u32[]{:S(2)}) copy-start(f32[1024,1568]{0,1:T(8,128)S(1)} %convolution_multiply_fusion) | copy-start | bytes 19267588
  11.4 9.3 %all-to-all-start = ((f32[2,4,256]{2,0,1:T(2,128)}), f32[2,4,256]{2,0,1:T(2,128)S(1)}, u32[]{:S(2)}, u32[]{:S(2)}) async-start(f32[2,4,256]{2,0,1:T(2,128)} %bitcast.2), calls=%async_computation | async-start | bytes 16384 | tf_op jit(solution)/shard_map/all_to_all | solution.py:101
  28.9 7.4 %all-to-all-start.1 = ((f32[2,4,256]{2,0,1:T(2,128)}), f32[2,4,256]{2,0,1:T(2,128)S(1)}, u32[]{:S(2)}, u32[]{:S(2)}) async-start(f32[2,4,256]{2,0,1:T(2,128)} %bitcast.6), calls=%async_computation.1 | async-start | bytes 16384 | tf_op jit(solution)/shard_map/all_to_all | solution.py:102
  58.2 29.4 %all-to-all-start.4 = ((f32[8,32,1,6,256]{4,1,3,2,0:T(8,128)}), f32[8,32,1,6,256]{4,1,3,2,0:T(8,128)S(1)}, u32[]{:S(2)}, u32[]{:S(2)}) async-start(f32[8,32,1,6,256]{4,1,3,2,0:T(8,128)} %broadcast_in_dim.128), calls=%async_computation.4 | async-start | bytes 3145728 | tf_op jit(solution)/shard_map/all_to_all | solution.py:19
  103.4 5.8 %copy-start.3 = (bf16[1568,512]{1,0:T(8,128)(2,1)S(1)}, bf16[1568,512]{1,0:T(8,128)(2,1)}, u32[]{:S(2)}) copy-start(bf16[1568,512]{1,0:T(8,128)(2,1)} %reshape_reshape.12) | copy-start | bytes 4816900
  107.5 1.7 %copy-start.2 = (bf16[1024,1568]{0,1:T(8,128)(2,1)}, bf16[1024,1568]{0,1:T(8,128)(2,1)S(1)}, u32[]{:S(2)}) copy-start(bf16[1024,1568]{0,1:T(8,128)(2,1)S(1)} %fusion.1) | copy-start | bytes 9633796
  116.3 30.1 %all-to-all-start.5 = ((f32[8,32,4,512]{3,2,1,0:T(4,128)}), f32[8,32,4,512]{3,2,1,0:T(4,128)S(1)}, u32[]{:S(2)}, u32[]{:S(2)}) async-start(f32[8,32,4,512]{3,2,1,0:T(4,128)} %bitcast.101), calls=%async_computation.5 | async-start | bytes 4194304 | tf_op jit(solution)/shard_map/all_to_all | solution.py:52
  147.6 15.7 %all-to-all-start.6 = ((f32[32,4,512]{2,1,0:T(4,128)}), f32[32,4,512]{2,1,0:T(4,128)S(1)}, u32[]{:S(2)}, u32[]{:S(2)}) async-start(f32[32,4,512]{2,1,0:T(4,128)} %reduce_sum.131), calls=%async_computation.6 | async-start | bytes 524288 | tf_op jit(solution)/shard_map/all_to_all | solution.py:60
where the time goes:
time: 166 us; the launch traced here: 165 us
  waiting for transfers between devices  50.7 us (31%)
  blocking collectives  28.4 us (17%)
  local copies, waits for them, and re-layouts  26.2 us (16%)
  starting transfers between devices  25.1 us (15%)
  other arithmetic  19.6 us (12%)
  matrix products  11.6 us (7%)
  between operations  3.36 us (2%)
    all_to_all x1, waiting for transfers between devices, sum_at_owner(): lax.all_to_all(blocks, axis, split_axis=0, concat_axis=0, tiled=True)  26.2 us
    all_to_all x1, waiting for transfers between devices, sent_to_all(): lax.all_to_all(jnp.broadcast_to(value[None], (peers, *value.shape)), axis...  20.5 us
    all_to_all x1, blocking collectives, sent_to_all(): lax.all_to_all(jnp.broadcast_to(value[None], (peers, *value.shape)), axis...  20.2 us
    all_to_all x1, starting transfers between devices, sent_to_all(): lax.all_to_all(jnp.broadcast_to(value[None], (peers, *value.shape)), axis...  8.75 us
    all_to_all x1, blocking collectives, per_device(): lax.all_to_all(weighted.T, 'cap', split_axis=1, concat_axis=0, tiled=True)  8.2 us
    unnamed x13, local copies, waits for them, and re-layouts  6.95 us
    another operation x1, local copies, waits for them, and re-layouts, per_device(): similar = jnp.mean(all_pool.reshape(clip_total, clip_total, WORDS), axis=2)  6.13 us
    reduce_sum x1, other arithmetic, per_device(): similar = jnp.mean(all_pool.reshape(clip_total, clip_total, WORDS), axis=2)  5.61 us
  transfers between devices with their start and end apart: 5, of which 3 were waited for; matrix products, arithmetic and copies ran while one was open for 9% of the time, Pallas kernels for 0%

commit v1 on v0

v1 whole, which is shorter than its diff:
```python
import jax
import jax.numpy as jnp
from jax import lax
from jax.experimental import pallas as pl
from jax.experimental.pallas import tpu as pltpu
from jax.sharding import Mesh
from jax.sharding import PartitionSpec as P

XS, ZS, CS, YS = 4, 8, 2, 4
WORDS = 8
ROWS = 1024
DIM = 512
FRAMES = 16
PATCH = 49
CLIP_ROWS = FRAMES * PATCH
CAPS = 128
CHUNK = 256
HALF = 512
BLOCK = 128
SCALE = DIM**-0.5
LOG2E = 1.4426950408889634
LN2 = 0.6931471805599453
BIG = 1e30
LOGIT_SCALE = 32.0
LOSS_SCALE = 8192.0
NT = (((1,), (1,)), ((), ()))
NN = (((1,), (0,)), ((), ()))


def mm(a, b, dims):
    return lax.dot_general(a, b, dims, preferred_element_type=jnp.float32)


def three_parts(value):
    first = value.astype(jnp.bfloat16)
    rest = value - first.astype(jnp.float32)
    second = rest.astype(jnp.bfloat16)
    third = (rest - second.astype(jnp.float32)).astype(jnp.bfloat16)
    return jnp.concatenate([first, second, third], axis=0)


def added_parts(value, rows):
    return value[:rows] + value[rows : 2 * rows] + value[2 * rows : 3 * rows]


def kernel(
    text_hbm, patch_hbm, slots_ref,
    loss_ref, pg_ref, tg_ref,
    text_in, text_wide, text_perm, patch, patch_t, bias_ref, member,
    z_ref, gh_ref, cap_rx, near_rx, far_rx,
    t_own, t_send, t_recv, coef_ref,
    snd1, own1, rcv1, snd2, own2, rcv2, sum2, snd3, own3, rcv3, pg_buf, gs_ref,
    text_sem, patch_sem, pg_sem,
    cap_ss, cap_rs, near_ss, near_rs, far_ss, far_rs, core_ss, core_rs,
    ss1, rs1, ss2, rs2, ss3, rs3,
):
    x = lax.axis_index("x")
    z = lax.axis_index("z")
    core = lax.axis_index("core")
    y = lax.axis_index("y")
    xc = x * CS + core

    text_copy = pltpu.make_async_copy(text_hbm, text_in, text_sem)
    text_copy.start()
    patch_copies = []
    for v in range(2):
        rows = pl.ds(v * CLIP_ROWS, CLIP_ROWS)
        copy = pltpu.make_async_copy(patch_hbm.at[rows], patch.at[rows], patch_sem.at[v])
        copy.start()
        patch_copies.append(copy)

    def near_peer(i):
        other = lax.rem(xc + i, XS * CS)
        return (other // CS, z, lax.rem(other, CS), y)

    def far_peer(i):
        return (x, lax.rem(z + i, ZS), core, y)

    def cap_peer(i):
        return (x, z, core, lax.rem(y + i, YS))

    barrier = pltpu.get_barrier_semaphore()
    peers = [near_peer(i) for i in range(1, XS * CS)]
    peers += [far_peer(i) for i in range(1, ZS)]
    peers += [cap_peer(i) for i in range(1, YS)]
    for peer in peers:
        pl.semaphore_signal(barrier, inc=1, device_id=peer, device_id_type=pl.DeviceIdType.MESH)

    slots = slots_ref[...]
    at_row = lax.broadcasted_iota(jnp.int32, (FRAMES, FRAMES), 0)
    at_col = lax.broadcasted_iota(jnp.int32, (FRAMES, FRAMES), 1)
    for v in range(2):
        usable = jnp.where(slots[v : v + 1] >= 0, 0.0, -BIG)
        spread = jnp.where(at_row == at_col, jnp.broadcast_to(usable, (FRAMES, FRAMES)), 0.0)
        column = jnp.sum(spread, axis=1, keepdims=True)
        bias_ref[v] = jnp.broadcast_to(column, (FRAMES, BLOCK))

    q = lax.broadcasted_iota(jnp.int32, (ROWS, CAPS), 0)
    c = lax.broadcasted_iota(jnp.int32, (ROWS, CAPS), 1)
    qh, q1, q2, qz = q // 512, (q // 128) % 4, (q // 8) % 4, q % 8
    qy = jnp.where(qh == 0, q1, q2)
    qx = jnp.where(qh == 0, q2, q1)
    caption = qx * 32 + qz * 4 + qh * 2 + qy // 2
    member[...] = jnp.where(caption == c, 1.0, 0.0).astype(jnp.bfloat16)

    text_copy.wait()
    for j in range(4):
        text_wide[j] = text_in[:, j * BLOCK : (j + 1) * BLOCK].astype(jnp.float32)
    for h in range(2):
        for b1 in range(4):
            for k in range(4):
                base = h * 512 + b1 * 128 + k * 32
                for j in range(4):
                    pieces = []
                    for b2 in range(4):
                        fx, fy = (b2, b1) if h == 0 else (b1, b2)
                        start = fx * 256 + h * 16 + fy * 4 + k
                        pieces.append(text_wide[j, pl.ds(start, 8, stride=32), :])
                    group = jnp.concatenate(pieces, axis=0).astype(jnp.bfloat16)
                    text_perm[base : base + 32, j * BLOCK : (j + 1) * BLOCK] = group

    def tiled(value):
        return jnp.broadcast_to(value, (FRAMES, CHUNK))

    def wide_bias(v):
        part = bias_ref[v]
        return jnp.concatenate([part, part], axis=1)

    def forward(i, _):
        v, n = i // 4, i % 4
        scores = mm(
            patch[pl.ds(pl.multiple_of(v * CLIP_ROWS, 16), CLIP_ROWS), :],
            text_perm[pl.ds(pl.multiple_of(n * CHUNK, CHUNK), CHUNK), :],
            NT,
        )
        z_ref[i] = scores
        top = z_ref[i, 0:FRAMES, :]
        for p in range(1, PATCH):
            top = jnp.maximum(top, z_ref[i, p * FRAMES : (p + 1) * FRAMES, :])
        bias = wide_bias(v)
        peak = jnp.max(top + bias, axis=0, keepdims=True) * (SCALE * LOG2E)
        offset = bias - tiled(peak)
        total = jnp.zeros((FRAMES, CHUNK), jnp.float32)
        weighted = jnp.zeros((FRAMES, CHUNK), jnp.float32)
        for p in range(PATCH):
            s = z_ref[i, p * FRAMES : (p + 1) * FRAMES, :]
            e = jnp.exp2(s * (SCALE * LOG2E) + offset)
            total = total + e
            weighted = weighted + e * s
        total = jnp.sum(total, axis=0, keepdims=True)
        weighted = jnp.sum(weighted, axis=0, keepdims=True)
        lanes = pl.ds(pl.multiple_of(n * CHUNK, CHUNK), CHUNK)
        cap_rx[y, v, 0:1, lanes] = peak + jnp.log(total) * LOG2E
        cap_rx[y, v, 1:2, lanes] = weighted * SCALE / total
        return 0

    patch_copies[0].wait()
    patch_copies[1].wait()
    lax.fori_loop(0, 8, forward, 0)

    pl.semaphore_wait(barrier, len(peers))

    cap_copies = []
    for i in range(1, YS):
        copy = pltpu.make_async_remote_copy(
            src_ref=cap_rx.at[y], dst_ref=cap_rx.at[y],
            send_sem=cap_ss.at[i - 1], recv_sem=cap_rs.at[i - 1],
            device_id=cap_peer(i), device_id_type=pl.DeviceIdType.MESH,
        )
        copy.start()
        cap_copies.append(copy)

    for v in range(2):
        patch_t[v] = patch[v * CLIP_ROWS : (v + 1) * CLIP_ROWS, :].T

    for copy in cap_copies:
        copy.wait()

    lse, pooled = [], []
    for v in range(2):
        parts = [cap_rx[j, v, 0:1, :] for j in range(YS)]
        top = jnp.maximum(jnp.maximum(parts[0], parts[1]), jnp.maximum(parts[2], parts[3]))
        factors = [jnp.exp2(part - top) for part in parts]
        total = factors[0] + factors[1] + factors[2] + factors[3]
        mean = factors[0] * cap_rx[0, v, 1:2, :]
        for j in range(1, YS):
            mean = mean + factors[j] * cap_rx[j, v, 1:2, :]
        pooled.append(mean / total)
        lse.append(top + jnp.log(total) * LOG2E)
    both = jnp.concatenate(pooled, axis=0)
    logits_own = added_parts(mm(three_parts(both), member[...], NN), 2) * (LOGIT_SCALE / WORDS)
    near_rx[xc] = logits_own
    near_copies = []
    for i in range(1, XS * CS):
        copy = pltpu.make_async_remote_copy(
            src_ref=near_rx.at[xc], dst_ref=near_rx.at[xc],
            send_sem=near_ss.at[i - 1], recv_sem=near_rs.at[i - 1],
            device_id=near_peer(i), device_id_type=pl.DeviceIdType.MESH,
        )
        copy.start()
        near_copies.append(copy)

    for v in range(2):
        cap_rx[y, v, 0:1, :] = lse[v]
        cap_rx[y, v, 1:2, :] = 1.0 - pooled[v]

    def shaped(half):
        def body(i, _):
            v, m = i // 2, i % 2
            n = half * 2 + m
            lanes = pl.ds(pl.multiple_of(n * CHUNK, CHUNK), CHUNK)
            offset = wide_bias(v) - tiled(cap_rx[y, v, 0:1, lanes])
            shift = tiled(cap_rx[y, v, 1:2, lanes])
            inner = pl.ds(pl.multiple_of(m * CHUNK, CHUNK), CHUNK)
            j = v * 4 + n
            for p in range(PATCH):
                s = z_ref[j, p * FRAMES : (p + 1) * FRAMES, :]
                w = jnp.exp2(s * (SCALE * LOG2E) + offset)
                g = w * (s * SCALE + shift)
                gh_ref[v, half, p * FRAMES : (p + 1) * FRAMES, inner] = g.astype(jnp.bfloat16)
            return 0

        lax.fori_loop(0, 4, body, 0)

    other = 1 - core
    shaped(other)
    core_copies = []
    for v in range(2):
        t_send[v] = mm(patch_t[v], gh_ref[v, other], NN).astype(jnp.bfloat16)
        copy = pltpu.make_async_remote_copy(
            src_ref=t_send.at[v], dst_ref=t_recv.at[v],
            send_sem=core_ss.at[v], recv_sem=core_rs.at[v],
            device_id=(x, z, other, y), device_id_type=pl.DeviceIdType.MESH,
        )
        copy.start()
        core_copies.append(copy)

    for copy in near_copies:
        copy.wait()
    far_rx[z] = jnp.concatenate([near_rx[j] for j in range(XS * CS)], axis=0)
    far_copies = []
    for i in range(1, ZS):
        copy = pltpu.make_async_remote_copy(
            src_ref=far_rx.at[z], dst_ref=far_rx.at[z],
            send_sem=far_ss.at[i - 1], recv_sem=far_rs.at[i - 1],
            device_id=far_peer(i), device_id_type=pl.DeviceIdType.MESH,
        )
        copy.start()
        far_copies.append(copy)

    shaped(core)
    for v in range(2):
        t_own[v] = mm(patch_t[v], gh_ref[v, core], NN)

    for copy in far_copies:
        copy.wait()

    logits = jnp.concatenate([far_rx[j] for j in range(ZS)], axis=0)
    row = lax.broadcasted_iota(jnp.int32, (CAPS, CAPS), 0)
    col = lax.broadcasted_iota(jnp.int32, (CAPS, CAPS), 1)
    clip = ((row // 4) % 4) * 32 + (row // 16) * 4 + row % 4
    matched = jnp.sum(jnp.where(clip == col, logits, 0.0), axis=1, keepdims=True)
    cap_top = jnp.max(logits, axis=0, keepdims=True)
    cap_lse = cap_top + jnp.log(jnp.sum(jnp.exp(logits - cap_top), axis=0, keepdims=True))
    clip_top = jnp.max(logits, axis=1, keepdims=True)
    clip_lse = clip_top + jnp.log(jnp.sum(jnp.exp(logits - clip_top), axis=1, keepdims=True))
    terms = jnp.sum(cap_lse, axis=1, keepdims=True) + jnp.sum(clip_lse - 2.0 * matched, axis=0, keepdims=True)
    loss_ref[...] = terms * (0.5 / CAPS)

    near = jnp.concatenate([near_rx[xc], near_rx[x * CS + other]], axis=0)
    near_top = jnp.max(near, axis=1, keepdims=True)
    near_exp = jnp.exp(near - near_top)
    by_clip = near_exp / jnp.sum(near_exp, axis=1, keepdims=True)
    by_cap = jnp.exp(near - cap_lse)
    row = lax.broadcasted_iota(jnp.int32, (4, CAPS), 0)
    col = lax.broadcasted_iota(jnp.int32, (4, CAPS), 1)
    which = jnp.where(row < 2, core, other)
    mine = (x * ZS + z) * 4 + which * 2 + row % 2
    eye = jnp.where(mine == col, 1.0, 0.0)
    grad = (by_clip + by_cap - 2.0 * eye) * (LOSS_SCALE * 0.5 / CAPS * LOGIT_SCALE / WORDS * SCALE)
    coef = added_parts(mm(three_parts(grad), member[...], NT), 4)
    coef_ref[0] = coef[:, :HALF]
    coef_ref[1] = coef[:, HALF:]

    for copy in core_copies:
        copy.wait()

    first = y + core * (x - y)
    second = x + core * (y - x)

    def first_peer(b):
        return (x + core * (b - x), z, core, b + core * (y - b))

    def second_peer(b):
        return (b + core * (x - b), z, core, y + core * (b - y))

    copies1 = []
    for slot, i in enumerate((2, 1, 3, 0)):
        b = lax.rem(first + i, 4)
        lanes = pl.ds(pl.multiple_of(b * BLOCK, BLOCK), BLOCK)
        part = coef_ref[core, 0:1, lanes] * t_own[0, :, lanes]
        part = part + coef_ref[core, 1:2, lanes] * t_own[1, :, lanes]
        part = part + coef_ref[core, 2:3, lanes] * t_recv[0, :, lanes].astype(jnp.float32)
        part = part + coef_ref[core, 3:4, lanes] * t_recv[1, :, lanes].astype(jnp.float32)
        if i == 0:
            own1[...] = part
        else:
            snd1[slot] = part.astype(jnp.bfloat16)
            copy = pltpu.make_async_remote_copy(
                src_ref=snd1.at[slot], dst_ref=rcv1.at[slot],
                send_sem=ss1.at[slot], recv_sem=rs1.at[slot],
                device_id=first_peer(b), device_id_type=pl.DeviceIdType.MESH,
            )
            copy.start()
            copies1.append(copy)

    pg_copies = []
    for v in range(2):
        def scaled(p, _, v=v):
            rows = pl.ds(pl.multiple_of(p * 112, 16), 112)
            for h in range(2):
                g = gh_ref[v, h, rows, :].astype(jnp.float32) * coef_ref[h, v : v + 1, :]
                gs_ref[rows, h * HALF : (h + 1) * HALF] = g.astype(jnp.bfloat16)
            return 0

        lax.fori_loop(0, 7, scaled, 0)
        rows = pl.ds(v * CLIP_ROWS, CLIP_ROWS)
        pg_buf[rows, :] = mm(gs_ref[...], text_perm[...], NN).astype(jnp.bfloat16)
        copy = pltpu.make_async_copy(pg_buf.at[rows], pg_ref.at[rows], pg_sem.at[v])
        copy.start()
        pg_copies.append(copy)

    for copy in copies1:
        copy.wait()
    summed = own1[...]
    for slot in range(3):
        summed = summed + rcv1[slot].astype(jnp.float32)
    own2[...] = summed.T
    copies2 = []
    for slot, i in enumerate((2, 1, 3)):
        b = lax.rem(second + i, 4)
        part = jnp.concatenate(
            [own2[pl.ds(pl.multiple_of(k * 32 + b * 8, 8), 8), :] for k in range(4)], axis=0
        )
        snd2[slot] = part.astype(jnp.bfloat16)
        copy = pltpu.make_async_remote_copy(
            src_ref=snd2.at[slot], dst_ref=rcv2.at[slot],
            send_sem=ss2.at[slot], recv_sem=rs2.at[slot],
            device_id=second_peer(b), device_id_type=pl.DeviceIdType.MESH,
        )
        copy.start()
        copies2.append(copy)
    summed = jnp.concatenate(
        [own2[pl.ds(pl.multiple_of(k * 32 + second * 8, 8), 8), :] for k in range(4)], axis=0
    )
    for copy in copies2:
        copy.wait()
    for slot in range(3):
        summed = summed + rcv2[slot].astype(jnp.float32)
    for m in range(4):
        sum2[m] = summed[:, m * BLOCK : (m + 1) * BLOCK]
    for j in range(ZS):
        part = jnp.concatenate([sum2[m, pl.ds(j, 4, stride=8), :] for m in range(4)], axis=1)
        own3[j] = part
        snd3[j] = part.astype(jnp.bfloat16)
    copies3 = []
    for i in (4, 3, 5, 2, 6, 1, 7):
        b = lax.rem(z + i, ZS)
        copy = pltpu.make_async_remote_copy(
            src_ref=snd3.at[b], dst_ref=rcv3.at[i - 1],
            send_sem=ss3.at[i - 1], recv_sem=rs3.at[i - 1],
            device_id=far_peer(i), device_id_type=pl.DeviceIdType.MESH,
        )
        copy.start()
        copies3.append(copy)
    result = own3[z]
    for copy in copies3:
        copy.wait()
    for i in range(ZS - 1):
        result = result + rcv3[i].astype(jnp.float32)
    tg_ref[...] = result
    for copy in pg_copies:
        copy.wait()


def fused(text, patches, slots):
    f32, bf16 = jnp.float32, jnp.bfloat16
    vmem = pltpu.VMEM
    dma = pltpu.SemaphoreType.DMA
    return pl.pallas_call(
        kernel,
        out_shape=(
            jax.ShapeDtypeStruct((1, 1), f32),
            jax.ShapeDtypeStruct((2 * CLIP_ROWS, DIM), bf16),
            jax.ShapeDtypeStruct((4, DIM), f32),
        ),
        in_specs=[
            pl.BlockSpec(memory_space=pl.ANY),
            pl.BlockSpec(memory_space=pl.ANY),
            pl.BlockSpec(memory_space=vmem),
        ],
        out_specs=(
            pl.BlockSpec(memory_space=vmem),
            pl.BlockSpec(memory_space=pl.ANY),
            pl.BlockSpec(memory_space=vmem),
        ),
        scratch_shapes=[
            vmem((ROWS, DIM), bf16),
            vmem((4, ROWS, BLOCK), f32),
            vmem((ROWS, DIM), bf16),
            vmem((2 * CLIP_ROWS, DIM), bf16),
            vmem((2, DIM, CLIP_ROWS), bf16),
            vmem((2, FRAMES, BLOCK), f32),
            vmem((ROWS, CAPS), bf16),
            vmem((8, CLIP_ROWS, CHUNK), f32),
            vmem((2, 2, CLIP_ROWS, HALF), bf16),
            vmem((YS, 2, 2, ROWS), f32),
            vmem((XS * CS, 2, CAPS), f32),
            vmem((ZS, 16, CAPS), f32),
            vmem((2, DIM, HALF), f32),
            vmem((2, DIM, HALF), bf16),
            vmem((2, DIM, HALF), bf16),
            vmem((2, 4, HALF), f32),
            vmem((3, DIM, BLOCK), bf16),
            vmem((DIM, BLOCK), f32),
            vmem((3, DIM, BLOCK), bf16),
            vmem((3, 32, DIM), bf16),
            vmem((BLOCK, DIM), f32),
            vmem((3, 32, DIM), bf16),
            vmem((4, 32, BLOCK), f32),
            vmem((ZS, 4, DIM), bf16),
            vmem((ZS, 4, DIM), f32),
            vmem((ZS - 1, 4, DIM), bf16),
            vmem((2 * CLIP_ROWS, DIM), bf16),
            vmem((CLIP_ROWS, ROWS), bf16),
            dma, dma((2,)), dma((2,)),
            dma((3,)), dma((3,)), dma((7,)), dma((7,)), dma((7,)), dma((7,)), dma((2,)), dma((2,)),
            dma((3,)), dma((3,)), dma((3,)), dma((3,)), dma((7,)), dma((7,)),
        ],
        compiler_params=pltpu.CompilerParams(
            collective_id=0, has_side_effects=True, vmem_limit_bytes=52 * 1024 * 1024
        ),
    )(text, patches, slots)


def per_device(text, patches, frame_slots):
    flat = patches.transpose(0, 2, 1, 3).reshape(2 * CLIP_ROWS, DIM)
    loss, grad, text_grad = fused(text, flat, frame_slots)
    grad = grad.reshape(2, PATCH, FRAMES, DIM).transpose(0, 2, 1, 3)
    return loss.reshape(()), grad, text_grad


def solution(mesh):
    finer = Mesh(mesh.devices.reshape(XS, ZS, CS, YS), ("x", "z", "core", "y"))
    clip = ("x", "z", "core")
    in_specs = (P(), P(clip, None, "y", None), P(clip, None))
    out_specs = (P(), P(clip, None, "y", None), P((*clip, "y"), None))
    return jax.shard_map(
        per_device, mesh=finer, in_specs=in_specs, out_specs=out_specs, check_vma=False
    )
```

time: 166 us -> 47.4 us (0.29)
  the two profiles are of different devices: /device:TPU:1 before, /device:TPU:8 now
where the time goes in v1:
time: 47.4 us; the launch traced here: 47.2 us
  Pallas kernels  39.5 us (83%)
  local copies, waits for them, and re-layouts  5.19 us (11%)
  between operations  2.47 us (5%)
    pallas_call x1, Pallas kernels, fused(): pl.pallas_call(kernel, out_shape=(jax.ShapeDtypeStruct((1, 1), f32), jax....  39.5 us
    unnamed x6, local copies, waits for them, and re-layouts  5.19 us

profile of v1, /device:TPU:8, one launch (start us, length us, event | category | flops | bytes accessed | tf_op | source)
XLA Modules:
  0.0 47.2 jit_solution(2560250597296246120)
XLA Ops:
  0.6 0.0 copy-start
  0.6 1.2 %copy-done = bf16[1024,512]{1,0:T(8,128)(2,1)S(1)} copy-done((bf16[1024,512]{1,0:T(8,128)(2,1)S(1)}, bf16[1024,512]{1,0:T(8,128)(2,1)}, u32[]{:S(2)}) %copy-start) | copy-done | bytes 1048600
  1.9 0.0 copy-start.1
  1.9 0.7 %copy-done.1 = s32[2,16]{1,0:T(2,128)S(1)} copy-done((s32[2,16]{1,0:T(2,128)S(1)}, s32[2,16]{1,0:T(2,128)}, u32[]{:S(2)}) %copy-start.1) | copy-done | bytes 152
  2.5 39.5 %shard_map.58 = (f32[1,1]{1,0:T(1,128)}, bf16[1568,512]{1,0:T(8,128)(2,1)}, f32[4,512]{1,0:T(4,128)S(1)}) custom-call(bf16[1024,512]{1,0:T(8,128)(2,1)S(1)} %copy-done, bf16[1568,512]{1,0:T(8,128)(2,1)} %bitcast.7, s32[2,16]{1,0:T(2,128)S(1)} %copy-done.1), custom_call_target="tpu_custom_call" | custom-call | tf_op jit(solution)/shard_map/pallas_call | solution.py:390
  42.8 2.7 %copy.10 = bf16[2,16,49,512]{3,1,2,0:T(8,128)(2,1)} copy(bf16[2,16,49,512]{3,1,2,0:T(8,128)(2,1)} %bitcast.8) | data formatting | bytes 3211264
  45.5 0.6 %copy.11 = f32[4,512]{1,0:T(4,128)} copy(f32[4,512]{1,0:T(4,128)S(1)} %get-tuple-element.14) | data formatting | bytes 16384
Async XLA Ops:
  0.6 1.2 %copy-start = (bf16[1024,512]{1,0:T(8,128)(2,1)S(1)}, bf16[1024,512]{1,0:T(8,128)(2,1)}, u32[]{:S(2)}) copy-start(bf16[1024,512]{1,0:T(8,128)(2,1)} %text_hbm.1) | copy-start | bytes 3145732
  1.9 0.7 %copy-start.1 = (s32[2,16]{1,0:T(2,128)S(1)}, s32[2,16]{1,0:T(2,128)}, u32[]{:S(2)}) copy-start(s32[2,16]{1,0:T(2,128)} %slots_ref.1) | copy-start | bytes 388

commit v2 on v1

--- a/solution.py
+++ b/solution.py
@@ -23,8 +23,13 @@
 BIG = 1e30
 LOGIT_SCALE = 32.0
 LOSS_SCALE = 8192.0
+PLANE = sorted(
+    ((dx, dy) for dx in range(XS) for dy in range(YS) if dx or dy),
+    key=lambda d: (-min(d[0], XS - d[0]) - min(d[1], YS - d[1]), d),
+)
 NT = (((1,), (1,)), ((), ()))
 NN = (((1,), (0,)), ((), ()))
+TN = (((0,), (0,)), ((), ()))
 
 
 def mm(a, b, dims):
@@ -44,15 +49,15 @@
 
 
 def kernel(
-    text_hbm, patch_hbm, slots_ref,
+    text_hbm, patch_hbm, slots_hbm,
     loss_ref, pg_ref, tg_ref,
-    text_in, text_wide, text_perm, patch, patch_t, bias_ref, member,
+    text_in, text_wide, text_perm, patch, slots_ref, bias_ref, member,
     z_ref, gh_ref, cap_rx, near_rx, far_rx,
-    t_own, t_send, t_recv, coef_ref,
-    snd1, own1, rcv1, snd2, own2, rcv2, sum2, snd3, own3, rcv3, pg_buf, gs_ref,
-    text_sem, patch_sem, pg_sem,
+    t_own, t_send, t_recv, coef_ref, wide_coef,
+    snd1, rcv1, sum1, snd2, own2, rcv2, gs_ref,
+    text_sem, patch_sem, slots_sem,
     cap_ss, cap_rs, near_ss, near_rs, far_ss, far_rs, core_ss, core_rs,
-    ss1, rs1, ss2, rs2, ss3, rs3,
+    ss1, rs1, ss2, rs2,
 ):
     x = lax.axis_index("x")
     z = lax.axis_index("z")
@@ -68,6 +73,8 @@
         copy = pltpu.make_async_copy(patch_hbm.at[rows], patch.at[rows], patch_sem.at[v])
         copy.start()
         patch_copies.append(copy)
+    slots_copy = pltpu.make_async_copy(slots_hbm, slots_ref, slots_sem)
+    slots_copy.start()
 
     def near_peer(i):
         other = lax.rem(xc + i, XS * CS)
@@ -79,13 +86,17 @@
     def cap_peer(i):
         return (x, z, core, lax.rem(y + i, YS))
 
+    def plane_peer(dx, dy):
+        return (lax.rem(x + dx, XS), z, core, lax.rem(y + dy, YS))
+
     barrier = pltpu.get_barrier_semaphore()
     peers = [near_peer(i) for i in range(1, XS * CS)]
     peers += [far_peer(i) for i in range(1, ZS)]
-    peers += [cap_peer(i) for i in range(1, YS)]
+    peers += [plane_peer(dx, dy) for dx in range(XS) for dy in range(1, YS)]
     for peer in peers:
         pl.semaphore_signal(barrier, inc=1, device_id=peer, device_id_type=pl.DeviceIdType.MESH)
 
+    slots_copy.wait()
     slots = slots_ref[...]
     at_row = lax.broadcasted_iota(jnp.int32, (FRAMES, FRAMES), 0)
     at_col = lax.broadcasted_iota(jnp.int32, (FRAMES, FRAMES), 1)
@@ -97,9 +108,7 @@
 
     q = lax.broadcasted_iota(jnp.int32, (ROWS, CAPS), 0)
     c = lax.broadcasted_iota(jnp.int32, (ROWS, CAPS), 1)
-    qh, q1, q2, qz = q // 512, (q // 128) % 4, (q // 8) % 4, q % 8
-    qy = jnp.where(qh == 0, q1, q2)
-    qx = jnp.where(qh == 0, q2, q1)
+    qh, qx, qy, qz = q // 512, (q // 128) % 4, (q // 32) % 4, q % 8
     caption = qx * 32 + qz * 4 + qh * 2 + qy // 2
     member[...] = jnp.where(caption == c, 1.0, 0.0).astype(jnp.bfloat16)
 
@@ -107,14 +116,13 @@
     for j in range(4):
         text_wide[j] = text_in[:, j * BLOCK : (j + 1) * BLOCK].astype(jnp.float32)
     for h in range(2):
-        for b1 in range(4):
-            for k in range(4):
-                base = h * 512 + b1 * 128 + k * 32
+        for gx in range(4):
+            for gy in range(4):
+                base = h * 512 + gx * 128 + gy * 32
                 for j in range(4):
                     pieces = []
-                    for b2 in range(4):
-                        fx, fy = (b2, b1) if h == 0 else (b1, b2)
-                        start = fx * 256 + h * 16 + fy * 4 + k
+                    for k in range(4):
+                        start = gx * 256 + h * 16 + gy * 4 + k
                         pieces.append(text_wide[j, pl.ds(start, 8, stride=32), :])
                     group = jnp.concatenate(pieces, axis=0).astype(jnp.bfloat16)
                     text_perm[base : base + 32, j * BLOCK : (j + 1) * BLOCK] = group
@@ -126,14 +134,16 @@
         part = bias_ref[v]
         return jnp.concatenate([part, part], axis=1)
 
-    def forward(i, _):
+    def multiply(i):
         v, n = i // 4, i % 4
-        scores = mm(
-            patch[pl.ds(pl.multiple_of(v * CLIP_ROWS, 16), CLIP_ROWS), :],
-            text_perm[pl.ds(pl.multiple_of(n * CHUNK, CHUNK), CHUNK), :],
+        z_ref[i] = mm(
+            patch[v * CLIP_ROWS : (v + 1) * CLIP_ROWS, :],
+            text_perm[n * CHUNK : (n + 1) * CHUNK, :],
             NT,
         )
-        z_ref[i] = scores
+
+    def statistics(i):
+        v, n = i // 4, i % 4
         top = z_ref[i, 0:FRAMES, :]
         for p in range(1, PATCH):
             top = jnp.maximum(top, z_ref[i, p * FRAMES : (p + 1) * FRAMES, :])
@@ -149,14 +159,18 @@
             weighted = weighted + e * s
         total = jnp.sum(total, axis=0, keepdims=True)
         weighted = jnp.sum(weighted, axis=0, keepdims=True)
-        lanes = pl.ds(pl.multiple_of(n * CHUNK, CHUNK), CHUNK)
+        lanes = slice(n * CHUNK, (n + 1) * CHUNK)
         cap_rx[y, v, 0:1, lanes] = peak + jnp.log(total) * LOG2E
         cap_rx[y, v, 1:2, lanes] = weighted * SCALE / total
-        return 0
 
     patch_copies[0].wait()
-    patch_copies[1].wait()
-    lax.fori_loop(0, 8, forward, 0)
+    multiply(0)
+    for i in range(8):
+        if i == 3:
+            patch_copies[1].wait()
+        if i < 7:
+            multiply(i + 1)
+        statistics(i)
 
     pl.semaphore_wait(barrier, len(peers))
 
@@ -169,9 +183,6 @@
         )
         copy.start()
         cap_copies.append(copy)
-
-    for v in range(2):
-        patch_t[v] = patch[v * CLIP_ROWS : (v + 1) * CLIP_ROWS, :].T
 
     for copy in cap_copies:
         copy.wait()
@@ -226,7 +237,8 @@
     shaped(other)
     core_copies = []
     for v in range(2):
-        t_send[v] = mm(patch_t[v], gh_ref[v, other], NN).astype(jnp.bfloat16)
+        clip_patch = patch[v * CLIP_ROWS : (v + 1) * CLIP_ROWS, :]
+        t_send[v] = mm(gh_ref[v, other], clip_patch, TN).astype(jnp.bfloat16)
         copy = pltpu.make_async_remote_copy(
             src_ref=t_send.at[v], dst_ref=t_recv.at[v],
             send_sem=core_ss.at[v], recv_sem=core_rs.at[v],
@@ -250,7 +262,7 @@
 
     shaped(core)
     for v in range(2):
-        t_own[v] = mm(patch_t[v], gh_ref[v, core], NN)
+        t_own[v] = mm(gh_ref[v, core], patch[v * CLIP_ROWS : (v + 1) * CLIP_ROWS, :], TN)
 
     for copy in far_copies:
         copy.wait()
@@ -278,43 +290,48 @@
     mine = (x * ZS + z) * 4 + which * 2 + row % 2
     eye = jnp.where(mine == col, 1.0, 0.0)
     grad = (by_clip + by_cap - 2.0 * eye) * (LOSS_SCALE * 0.5 / CAPS * LOGIT_SCALE / WORDS * SCALE)
-    coef = added_parts(mm(three_parts(grad), member[...], NT), 4)
+    parts = three_parts(grad)
+    spread = jnp.concatenate(
+        [
+            jnp.concatenate(
+                [jnp.broadcast_to(parts[4 * t + j : 4 * t + j + 1], (BLOCK, CAPS)) for j in range(4)], axis=0
+            )
+            for t in range(3)
+        ],
+        axis=1,
+    )
+    of_half = member[pl.ds(pl.multiple_of(core * HALF, HALF), HALF), :]
+    wide_coef[...] = mm(jnp.concatenate([of_half, of_half, of_half], axis=1), spread, NT)
+
+    for copy in core_copies:
+        copy.wait()
+
+    def combined(dx, dy):
+        block = lax.rem(x + dx, XS) * YS + lax.rem(y + dy, YS)
+        rows = pl.ds(pl.multiple_of(block * 32, 32), 32)
+        part = jnp.zeros((32, DIM), jnp.float32)
+        for j in range(4):
+            factor = wide_coef[rows, j * BLOCK : (j + 1) * BLOCK]
+            factor = jnp.concatenate([factor] * 4, axis=1)
+            source = t_own[j, rows, :] if j < 2 else t_recv[j - 2, rows, :].astype(jnp.float32)
+            part = part + factor * source
+        return part
+
+    copies1 = []
+    for slot, (dx, dy) in enumerate(PLANE):
+        snd1[slot] = combined(dx, dy).astype(jnp.bfloat16)
+        copy = pltpu.make_async_remote_copy(
+            src_ref=snd1.at[slot], dst_ref=rcv1.at[slot],
+            send_sem=ss1.at[slot], recv_sem=rs1.at[slot],
+            device_id=plane_peer(dx, dy), device_id_type=pl.DeviceIdType.MESH,
+        )
+        copy.start()
+        copies1.append(copy)
+    sum1[...] = combined(0, 0)
+
+    coef = added_parts(mm(parts, member[...], NT), 4)
     coef_ref[0] = coef[:, :HALF]
     coef_ref[1] = coef[:, HALF:]
-
-    for copy in core_copies:
-        copy.wait()
-
-    first = y + core * (x - y)
-    second = x + core * (y - x)
-
-    def first_peer(b):
-        return (x + core * (b - x), z, core, b + core * (y - b))
-
-    def second_peer(b):
-        return (b + core * (x - b), z, core, y + core * (b - y))
-
-    copies1 = []
-    for slot, i in enumerate((2, 1, 3, 0)):
-        b = lax.rem(first + i, 4)
-        lanes = pl.ds(pl.multiple_of(b * BLOCK, BLOCK), BLOCK)
-        part = coef_ref[core, 0:1, lanes] * t_own[0, :, lanes]
-        part = part + coef_ref[core, 1:2, lanes] * t_own[1, :, lanes]
-        part = part + coef_ref[core, 2:3, lanes] * t_recv[0, :, lanes].astype(jnp.float32)
-        part = part + coef_ref[core, 3:4, lanes] * t_recv[1, :, lanes].astype(jnp.float32)
-        if i == 0:
-            own1[...] = part
-        else:
-            snd1[slot] = part.astype(jnp.bfloat16)
-            copy = pltpu.make_async_remote_copy(
-                src_ref=snd1.at[slot], dst_ref=rcv1.at[slot],
-                send_sem=ss1.at[slot], recv_sem=rs1.at[slot],
-                device_id=first_peer(b), device_id_type=pl.DeviceIdType.MESH,
-            )
-            copy.start()
-            copies1.append(copy)
-
-    pg_copies = []
     for v in range(2):
         def scaled(p, _, v=v):
             rows = pl.ds(pl.multiple_of(p * 112, 16), 112)
@@ -325,61 +342,45 @@
 
         lax.fori_loop(0, 7, scaled, 0)
         rows = pl.ds(v * CLIP_ROWS, CLIP_ROWS)
-        pg_buf[rows, :] = mm(gs_ref[...], text_perm[...], NN).astype(jnp.bfloat16)
-        copy = pltpu.make_async_copy(pg_buf.at[rows], pg_ref.at[rows], pg_sem.at[v])
-        copy.start()
-        pg_copies.append(copy)
+        pg_ref[rows, :] = mm(gs_ref[...], text_perm[...], NN).astype(jnp.bfloat16)
 
     for copy in copies1:
         copy.wait()
-    summed = own1[...]
-    for slot in range(3):
+    summed = sum1[...]
+    for slot in range(len(PLANE)):
         summed = summed + rcv1[slot].astype(jnp.float32)
-    own2[...] = summed.T
+    for m in range(4):
+        own2[m] = summed[:, m * BLOCK : (m + 1) * BLOCK]
+    for j in range(ZS):
+        part = jnp.concatenate([own2[m, pl.ds(j, 4, stride=8), :] for m in range(4)], axis=1)
+        snd2[j] = part
     copies2 = []
-    for slot, i in enumerate((2, 1, 3)):
-        b = lax.rem(second + i, 4)
-        part = jnp.concatenate(
-            [own2[pl.ds(pl.multiple_of(k * 32 + b * 8, 8), 8), :] for k in range(4)], axis=0
-        )
-        snd2[slot] = part.astype(jnp.bfloat16)
-        copy = pltpu.make_async_remote_copy(
-            src_ref=snd2.at[slot], dst_ref=rcv2.at[slot],
-            send_sem=ss2.at[slot], recv_sem=rs2.at[slot],
-            device_id=second_peer(b), device_id_type=pl.DeviceIdType.MESH,
-        )
-        copy.start()
-        copies2.append(copy)
-    summed = jnp.concatenate(
-        [own2[pl.ds(pl.multiple_of(k * 32 + second * 8, 8), 8), :] for k in range(4)], axis=0
-    )
-    for copy in copies2:
-        copy.wait()
-    for slot in range(3):
-        summed = summed + rcv2[slot].astype(jnp.float32)
-    for m in range(4):
-        sum2[m] = summed[:, m * BLOCK : (m + 1) * BLOCK]
-    for j in range(ZS):
-        part = jnp.concatenate([sum2[m, pl.ds(j, 4, stride=8), :] for m in range(4)], axis=1)
-        own3[j] = part
-        snd3[j] = part.astype(jnp.bfloat16)
-    copies3 = []
     for i in (4, 3, 5, 2, 6, 1, 7):
         b = lax.rem(z + i, ZS)
         copy = pltpu.make_async_remote_copy(
-            src_ref=snd3.at[b], dst_ref=rcv3.at[i - 1],
-            send_sem=ss3.at[i - 1], recv_sem=rs3.at[i - 1],
+            src_ref=snd2.at[b], dst_ref=rcv2.at[i - 1],
+            send_sem=ss2.at[i - 1], recv_sem=rs2.at[i - 1],
             device_id=far_peer(i), device_id_type=pl.DeviceIdType.MESH,
         )
         copy.start()
-        copies3.append(copy)
-    result = own3[z]
-    for copy in copies3:
+        copies2.append(copy)
+    result = snd2[z]
+    for copy in copies2:
         copy.wait()
     for i in range(ZS - 1):
-        result = result + rcv3[i].astype(jnp.float32)
+        result = result + rcv2[i]
     tg_ref[...] = result
-    for copy in pg_copies:
+
+
+def store(loss_in, pg_in, tg_in, loss_out, pg_out, tg_out, sems):
+    copies = [
+        pltpu.make_async_copy(pg_in, pg_out, sems.at[0]),
+        pltpu.make_async_copy(tg_in, tg_out, sems.at[1]),
+        pltpu.make_async_copy(loss_in, loss_out, sems.at[2]),
+    ]
+    for copy in copies:
+        copy.start()
+    for copy in copies:
         copy.wait()
 
 
@@ -387,29 +388,22 @@
     f32, bf16 = jnp.float32, jnp.bfloat16
     vmem = pltpu.VMEM
     dma = pltpu.SemaphoreType.DMA
-    return pl.pallas_call(
+    shapes = (
+        jax.ShapeDtypeStruct((1, 1), f32),
+        jax.ShapeDtypeStruct((2 * CLIP_ROWS, DIM), bf16),
+        jax.ShapeDtypeStruct((4, DIM), f32),
+    )
+    results = pl.pallas_call(
         kernel,
-        out_shape=(
-            jax.ShapeDtypeStruct((1, 1), f32),
-            jax.ShapeDtypeStruct((2 * CLIP_ROWS, DIM), bf16),
-            jax.ShapeDtypeStruct((4, DIM), f32),
-        ),
-        in_specs=[
-            pl.BlockSpec(memory_space=pl.ANY),
-            pl.BlockSpec(memory_space=pl.ANY),
-            pl.BlockSpec(memory_space=vmem),
-        ],
-        out_specs=(
-            pl.BlockSpec(memory_space=vmem),
-            pl.BlockSpec(memory_space=pl.ANY),
-            pl.BlockSpec(memory_space=vmem),
-        ),
+        out_shape=shapes,
+        in_specs=[pl.BlockSpec(memory_space=pltpu.HBM)] * 3,
+        out_specs=(pl.BlockSpec(memory_space=vmem),) * 3,
         scratch_shapes=[
             vmem((ROWS, DIM), bf16),
             vmem((4, ROWS, BLOCK), f32),
             vmem((ROWS, DIM), bf16),
             vmem((2 * CLIP_ROWS, DIM), bf16),
-            vmem((2, DIM, CLIP_ROWS), bf16),
+            vmem((2, FRAMES), jnp.int32),
             vmem((2, FRAMES, BLOCK), f32),
             vmem((ROWS, CAPS), bf16),
             vmem((8, CLIP_ROWS, CHUNK), f32),
@@ -417,30 +411,33 @@
             vmem((YS, 2, 2, ROWS), f32),
             vmem((XS * CS, 2, CAPS), f32),
             vmem((ZS, 16, CAPS), f32),
-            vmem((2, DIM, HALF), f32),
-            vmem((2, DIM, HALF), bf16),
-            vmem((2, DIM, HALF), bf16),
+            vmem((2, HALF, DIM), f32),
+            vmem((2, HALF, DIM), bf16),
+            vmem((2, HALF, DIM), bf16),
             vmem((2, 4, HALF), f32),
-            vmem((3, DIM, BLOCK), bf16),
-            vmem((DIM, BLOCK), f32),
-            vmem((3, DIM, BLOCK), bf16),
-            vmem((3, 32, DIM), bf16),
-            vmem((BLOCK, DIM), f32),
-            vmem((3, 32, DIM), bf16),
+            vmem((HALF, 4 * BLOCK), f32),
+            vmem((15, 32, DIM), bf16),
+            vmem((15, 32, DIM), bf16),
+            vmem((32, DIM), f32),
+            vmem((ZS, 4, DIM), f32),
             vmem((4, 32, BLOCK), f32),
-            vmem((ZS, 4, DIM), bf16),
-            vmem((ZS, 4, DIM), f32),
-            vmem((ZS - 1, 4, DIM), bf16),
-            vmem((2 * CLIP_ROWS, DIM), bf16),
+            vmem((ZS - 1, 4, DIM), f32),
             vmem((CLIP_ROWS, ROWS), bf16),
-            dma, dma((2,)), dma((2,)),
+            dma, dma((2,)), dma,
             dma((3,)), dma((3,)), dma((7,)), dma((7,)), dma((7,)), dma((7,)), dma((2,)), dma((2,)),
-            dma((3,)), dma((3,)), dma((3,)), dma((3,)), dma((7,)), dma((7,)),
+            dma((15,)), dma((15,)), dma((7,)), dma((7,)),
         ],
         compiler_params=pltpu.CompilerParams(
-            collective_id=0, has_side_effects=True, vmem_limit_bytes=52 * 1024 * 1024
+            collective_id=0, has_side_effects=True, vmem_limit_bytes=44 * 1024 * 1024
         ),
-    )(text, patches, slots)
+    )(*[pltpu.with_memory_space_constraint(a, pltpu.HBM) for a in (text, patches, slots)])
+    return pl.pallas_call(
+        store,
+        out_shape=shapes,
+        in_specs=[pl.BlockSpec(memory_space=pl.ANY)] * 3,
+        out_specs=(pl.BlockSpec(memory_space=pl.ANY),) * 3,
+        scratch_shapes=[dma((3,))],
+    )(*[pltpu.with_memory_space_constraint(a, pltpu.VMEM) for a in results])
 
 
 def per_device(text, patches, frame_slots):

time: 47.4 us -> 40.2 us (0.85)
  the two profiles are of different devices: /device:TPU:8 before, /device:TPU:1 now
where the time goes in v2:
time: 40.2 us; the launch traced here: 40 us
  Pallas kernels  39.4 us (98%)
  between operations  0.64 us (2%)
    pallas_call x1, Pallas kernels, fused(): pl.pallas_call(kernel, out_shape=shapes, in_specs=[pl.BlockSpec(memory_sp...  37.5 us
    pallas_call x1, Pallas kernels, fused(): pl.pallas_call(store, out_shape=shapes, in_specs=[pl.BlockSpec(memory_spa...  1.82 us

profile of v2, /device:TPU:1, one launch (start us, length us, event | category | flops | bytes accessed | tf_op | source)
XLA Modules:
  0.0 40.0 jit_solution(8457807556216443265)
XLA Ops:
  0.6 37.5 %shard_map.58 = (f32[1,1]{1,0:T(1,128)}, bf16[1568,512]{1,0:T(8,128)(2,1)S(1)}, f32[4,512]{1,0:T(4,128)S(1)}) custom-call(bf16[1024,512]{1,0:T(8,128)(2,1)} %text_hbm.1, bf16[1568,512]{1,0:T(8,128)(2,1)} %bitcast.7, s32[2,16]{1,0:T(2,128)} %slots_hbm.1), custom_call_target="tpu_custom_call" | custom-call | tf_op jit(solution)/shard_map/pallas_call | solution.py:396
  38.2 1.8 %shard_map.59 = (f32[1,1]{1,0:T(1,128)}, bf16[1568,512]{1,0:T(8,128)(2,1)}, f32[4,512]{1,0:T(4,128)}) custom-call(f32[1,1]{1,0:T(1,128)} %get-tuple-element.9.loss_in, bf16[1568,512]{1,0:T(8,128)(2,1)S(1)} %get-tuple-element.10.pg_in, f32[4,512]{1,0:T(4,128)S(1)} %get-tuple-element.11.tg_in), custom_call_target="tpu_custom_call" | custom-call | tf_op jit(solution)/shard_map/pallas_call | solution.py:434

commit v3 on v2

--- a/solution.py
+++ b/solution.py
@@ -23,6 +23,11 @@
 BIG = 1e30
 LOGIT_SCALE = 32.0
 LOSS_SCALE = 8192.0
+CHIP_COUNT = XS * ZS
+CHIPS = sorted(
+    ((dx, dz) for dx in range(XS) for dz in range(ZS) if dx or dz),
+    key=lambda d: (-min(d[0], XS - d[0]) - min(d[1], ZS - d[1]), d),
+)
 PLANE = sorted(
     ((dx, dy) for dx in range(XS) for dy in range(YS) if dx or dy),
     key=lambda d: (-min(d[0], XS - d[0]) - min(d[1], YS - d[1]), d),
@@ -52,33 +57,39 @@
     text_hbm, patch_hbm, slots_hbm,
     loss_ref, pg_ref, tg_ref,
     text_in, text_wide, text_perm, patch, slots_ref, bias_ref, member,
-    z_ref, gh_ref, cap_rx, near_rx, far_rx,
+    z_ref, gh_ref, cap_rx, pair_rx, chip_rx,
     t_own, t_send, t_recv, coef_ref, wide_coef,
-    snd1, rcv1, sum1, snd2, own2, rcv2, gs_ref,
+    snd1, rcv1, sum1, snd2, own2, own3, rcv2, gs_ref,
     text_sem, patch_sem, slots_sem,
-    cap_ss, cap_rs, near_ss, near_rs, far_ss, far_rs, core_ss, core_rs,
+    cap_ss, cap_rs, pair_ss, pair_rs, chip_ss, chip_rs, core_ss, core_rs,
     ss1, rs1, ss2, rs2,
 ):
     x = lax.axis_index("x")
     z = lax.axis_index("z")
     core = lax.axis_index("core")
     y = lax.axis_index("y")
-    xc = x * CS + core
-
-    text_copy = pltpu.make_async_copy(text_hbm, text_in, text_sem)
-    text_copy.start()
-    patch_copies = []
-    for v in range(2):
+    other = 1 - core
+    chip = x * ZS + z
+
+    slots_copy = pltpu.make_async_copy(slots_hbm, slots_ref, slots_sem)
+    text_copies, patch_copies = [], []
+
+    def fetch_text(n):
+        rows = pl.ds(n * CHUNK, CHUNK)
+        text_copies.append(pltpu.make_async_copy(text_hbm.at[rows], text_in.at[rows], text_sem.at[n]))
+        text_copies[-1].start()
+
+    def fetch_patch(v):
         rows = pl.ds(v * CLIP_ROWS, CLIP_ROWS)
-        copy = pltpu.make_async_copy(patch_hbm.at[rows], patch.at[rows], patch_sem.at[v])
-        copy.start()
-        patch_copies.append(copy)
-    slots_copy = pltpu.make_async_copy(slots_hbm, slots_ref, slots_sem)
+        patch_copies.append(pltpu.make_async_copy(patch_hbm.at[rows], patch.at[rows], patch_sem.at[v]))
+        patch_copies[-1].start()
+
+    fetch_text(0)
     slots_copy.start()
-
-    def near_peer(i):
-        other = lax.rem(xc + i, XS * CS)
-        return (other // CS, z, lax.rem(other, CS), y)
+    fetch_patch(0)
+    for n in range(1, XS):
+        fetch_text(n)
+    fetch_patch(1)
 
     def far_peer(i):
         return (x, lax.rem(z + i, ZS), core, y)
@@ -89,40 +100,30 @@
     def plane_peer(dx, dy):
         return (lax.rem(x + dx, XS), z, core, lax.rem(y + dy, YS))
 
+    def chip_peer(dx, dz):
+        return (lax.rem(x + dx, XS), lax.rem(z + dz, ZS), core, y)
+
+    twin = (x, z, other, y)
+
     barrier = pltpu.get_barrier_semaphore()
-    peers = [near_peer(i) for i in range(1, XS * CS)]
-    peers += [far_peer(i) for i in range(1, ZS)]
-    peers += [plane_peer(dx, dy) for dx in range(XS) for dy in range(1, YS)]
+    peers = [chip_peer(dx, dz) for dx, dz in CHIPS]
+    peers += [plane_peer(dx, dy) for dx, dy in PLANE if dy]
+    peers.append(twin)
     for peer in peers:
         pl.semaphore_signal(barrier, inc=1, device_id=peer, device_id_type=pl.DeviceIdType.MESH)
 
-    slots_copy.wait()
-    slots = slots_ref[...]
-    at_row = lax.broadcasted_iota(jnp.int32, (FRAMES, FRAMES), 0)
-    at_col = lax.broadcasted_iota(jnp.int32, (FRAMES, FRAMES), 1)
-    for v in range(2):
-        usable = jnp.where(slots[v : v + 1] >= 0, 0.0, -BIG)
-        spread = jnp.where(at_row == at_col, jnp.broadcast_to(usable, (FRAMES, FRAMES)), 0.0)
-        column = jnp.sum(spread, axis=1, keepdims=True)
-        bias_ref[v] = jnp.broadcast_to(column, (FRAMES, BLOCK))
-
-    q = lax.broadcasted_iota(jnp.int32, (ROWS, CAPS), 0)
-    c = lax.broadcasted_iota(jnp.int32, (ROWS, CAPS), 1)
-    qh, qx, qy, qz = q // 512, (q // 128) % 4, (q // 32) % 4, q % 8
-    caption = qx * 32 + qz * 4 + qh * 2 + qy // 2
-    member[...] = jnp.where(caption == c, 1.0, 0.0).astype(jnp.bfloat16)
-
-    text_copy.wait()
-    for j in range(4):
-        text_wide[j] = text_in[:, j * BLOCK : (j + 1) * BLOCK].astype(jnp.float32)
-    for h in range(2):
-        for gx in range(4):
+    def arrange(gx):
+        text_copies[gx].wait()
+        rows = slice(gx * CHUNK, (gx + 1) * CHUNK)
+        for j in range(4):
+            text_wide[j, rows, :] = text_in[rows, j * BLOCK : (j + 1) * BLOCK].astype(jnp.float32)
+        for h in range(2):
             for gy in range(4):
-                base = h * 512 + gx * 128 + gy * 32
+                base = gx * CHUNK + h * BLOCK + gy * 32
                 for j in range(4):
                     pieces = []
                     for k in range(4):
-                        start = gx * 256 + h * 16 + gy * 4 + k
+                        start = gx * CHUNK + h * 16 + gy * 4 + k
                         pieces.append(text_wide[j, pl.ds(start, 8, stride=32), :])
                     group = jnp.concatenate(pieces, axis=0).astype(jnp.bfloat16)
                     text_perm[base : base + 32, j * BLOCK : (j + 1) * BLOCK] = group
@@ -163,9 +164,22 @@
         cap_rx[y, v, 0:1, lanes] = peak + jnp.log(total) * LOG2E
         cap_rx[y, v, 1:2, lanes] = weighted * SCALE / total
 
+    arrange(0)
+    slots_copy.wait()
+    slots = slots_ref[...]
+    at_row = lax.broadcasted_iota(jnp.int32, (FRAMES, FRAMES), 0)
+    at_col = lax.broadcasted_iota(jnp.int32, (FRAMES, FRAMES), 1)
+    for v in range(2):
+        usable = jnp.where(slots[v : v + 1] >= 0, 0.0, -BIG)
+        spread = jnp.where(at_row == at_col, jnp.broadcast_to(usable, (FRAMES, FRAMES)), 0.0)
+        column = jnp.sum(spread, axis=1, keepdims=True)
+        bias_ref[v] = jnp.broadcast_to(column, (FRAMES, BLOCK))
+
     patch_copies[0].wait()
     multiply(0)
     for i in range(8):
+        if i < 3:
+            arrange(i + 1)
         if i == 3:
             patch_copies[1].wait()
         if i < 7:
@@ -183,6 +197,12 @@
         )
         copy.start()
         cap_copies.append(copy)
+
+    q = lax.broadcasted_iota(jnp.int32, (ROWS, CAPS), 0)
+    c = lax.broadcasted_iota(jnp.int32, (ROWS, CAPS), 1)
+    qx, qh, qy, qz = q // 256, (q // 128) % 2, (q // 32) % 4, q % 8
+    caption = qx * 32 + qz * 4 + qh * 2 + qy // 2
+    member[...] = jnp.where(caption == c, 1.0, 0.0).astype(jnp.bfloat16)
 
     for copy in cap_copies:
         copy.wait()
@@ -200,32 +220,27 @@
         lse.append(top + jnp.log(total) * LOG2E)
     both = jnp.concatenate(pooled, axis=0)
     logits_own = added_parts(mm(three_parts(both), member[...], NN), 2) * (LOGIT_SCALE / WORDS)
-    near_rx[xc] = logits_own
-    near_copies = []
-    for i in range(1, XS * CS):
-        copy = pltpu.make_async_remote_copy(
-            src_ref=near_rx.at[xc], dst_ref=near_rx.at[xc],
-            send_sem=near_ss.at[i - 1], recv_sem=near_rs.at[i - 1],
-            device_id=near_peer(i), device_id_type=pl.DeviceIdType.MESH,
-        )
-        copy.start()
-        near_copies.append(copy)
+    pair_rx[core] = logits_own
+    pair_copy = pltpu.make_async_remote_copy(
+        src_ref=pair_rx.at[core], dst_ref=pair_rx.at[core],
+        send_sem=pair_ss, recv_sem=pair_rs,
+        device_id=twin, device_id_type=pl.DeviceIdType.MESH,
+    )
+    pair_copy.start()
 
     for v in range(2):
         cap_rx[y, v, 0:1, :] = lse[v]
         cap_rx[y, v, 1:2, :] = 1.0 - pooled[v]
 
-    def shaped(half):
-        def body(i, _):
-            v, m = i // 2, i % 2
-            n = half * 2 + m
-            lanes = pl.ds(pl.multiple_of(n * CHUNK, CHUNK), CHUNK)
-            offset = wide_bias(v) - tiled(cap_rx[y, v, 0:1, lanes])
-            shift = tiled(cap_rx[y, v, 1:2, lanes])
-            inner = pl.ds(pl.multiple_of(m * CHUNK, CHUNK), CHUNK)
-            j = v * 4 + n
+    def shaped(v, half):
+        def body(n, _):
+            lanes = pl.ds(pl.multiple_of(n * CHUNK + half * BLOCK, BLOCK), BLOCK)
+            near = pl.ds(pl.multiple_of(half * BLOCK, BLOCK), BLOCK)
+            inner = pl.ds(pl.multiple_of(n * BLOCK, BLOCK), BLOCK)
+            offset = bias_ref[v] - jnp.broadcast_to(cap_rx[y, v, 0:1, lanes], (FRAMES, BLOCK))
+            shift = jnp.broadcast_to(cap_rx[y, v, 1:2, lanes], (FRAMES, BLOCK))
             for p in range(PATCH):
-                s = z_ref[j, p * FRAMES : (p + 1) * FRAMES, :]
+                s = z_ref[v * 4 + n, p * FRAMES : (p + 1) * FRAMES, near]
                 w = jnp.exp2(s * (SCALE * LOG2E) + offset)
                 g = w * (s * SCALE + shift)
                 gh_ref[v, half, p * FRAMES : (p + 1) * FRAMES, inner] = g.astype(jnp.bfloat16)
@@ -233,62 +248,57 @@
 
         lax.fori_loop(0, 4, body, 0)
 
-    other = 1 - core
-    shaped(other)
+    shaped(0, other)
+    pair_copy.wait()
+    chip_rx[chip] = jnp.concatenate([pair_rx[0], pair_rx[1]], axis=0)
+    chip_copies = []
+    for slot, (dx, dz) in enumerate(CHIPS):
+        copy = pltpu.make_async_remote_copy(
+            src_ref=chip_rx.at[chip], dst_ref=chip_rx.at[chip],
+            send_sem=chip_ss.at[slot], recv_sem=chip_rs.at[slot],
+            device_id=chip_peer(dx, dz), device_id_type=pl.DeviceIdType.MESH,
+        )
+        copy.start()
+        chip_copies.append(copy)
+
     core_copies = []
     for v in range(2):
+        if v:
+            shaped(v, other)
         clip_patch = patch[v * CLIP_ROWS : (v + 1) * CLIP_ROWS, :]
         t_send[v] = mm(gh_ref[v, other], clip_patch, TN).astype(jnp.bfloat16)
         copy = pltpu.make_async_remote_copy(
             src_ref=t_send.at[v], dst_ref=t_recv.at[v],
             send_sem=core_ss.at[v], recv_sem=core_rs.at[v],
-            device_id=(x, z, other, y), device_id_type=pl.DeviceIdType.MESH,
+            device_id=twin, device_id_type=pl.DeviceIdType.MESH,
         )
         copy.start()
         core_copies.append(copy)
 
-    for copy in near_copies:
-        copy.wait()
-    far_rx[z] = jnp.concatenate([near_rx[j] for j in range(XS * CS)], axis=0)
-    far_copies = []
-    for i in range(1, ZS):
-        copy = pltpu.make_async_remote_copy(
-            src_ref=far_rx.at[z], dst_ref=far_rx.at[z],
-            send_sem=far_ss.at[i - 1], recv_sem=far_rs.at[i - 1],
-            device_id=far_peer(i), device_id_type=pl.DeviceIdType.MESH,
-        )
-        copy.start()
-        far_copies.append(copy)
-
-    shaped(core)
-    for v in range(2):
+    for v in range(2):
+        shaped(v, core)
         t_own[v] = mm(gh_ref[v, core], patch[v * CLIP_ROWS : (v + 1) * CLIP_ROWS, :], TN)
 
-    for copy in far_copies:
-        copy.wait()
-
-    logits = jnp.concatenate([far_rx[j] for j in range(ZS)], axis=0)
-    row = lax.broadcasted_iota(jnp.int32, (CAPS, CAPS), 0)
-    col = lax.broadcasted_iota(jnp.int32, (CAPS, CAPS), 1)
-    clip = ((row // 4) % 4) * 32 + (row // 16) * 4 + row % 4
-    matched = jnp.sum(jnp.where(clip == col, logits, 0.0), axis=1, keepdims=True)
-    cap_top = jnp.max(logits, axis=0, keepdims=True)
-    cap_lse = cap_top + jnp.log(jnp.sum(jnp.exp(logits - cap_top), axis=0, keepdims=True))
-    clip_top = jnp.max(logits, axis=1, keepdims=True)
-    clip_lse = clip_top + jnp.log(jnp.sum(jnp.exp(logits - clip_top), axis=1, keepdims=True))
-    terms = jnp.sum(cap_lse, axis=1, keepdims=True) + jnp.sum(clip_lse - 2.0 * matched, axis=0, keepdims=True)
-    loss_ref[...] = terms * (0.5 / CAPS)
-
-    near = jnp.concatenate([near_rx[xc], near_rx[x * CS + other]], axis=0)
+    for copy in chip_copies:
+        copy.wait()
+
+    blocks = [chip_rx[j] for j in range(CHIP_COUNT)]
+    cap_top = blocks[0]
+    for block in blocks[1:]:
+        cap_top = jnp.maximum(cap_top, block)
+    cap_top = jnp.max(cap_top, axis=0, keepdims=True)
+    cap_sum = jnp.exp(blocks[0] - cap_top)
+    for block in blocks[1:]:
+        cap_sum = cap_sum + jnp.exp(block - cap_top)
+    cap_lse = cap_top + jnp.log(jnp.sum(cap_sum, axis=0, keepdims=True))
+    row = lax.broadcasted_iota(jnp.int32, (4, CAPS), 0)
+    col = lax.broadcasted_iota(jnp.int32, (4, CAPS), 1)
+    near = chip_rx[chip]
     near_top = jnp.max(near, axis=1, keepdims=True)
     near_exp = jnp.exp(near - near_top)
     by_clip = near_exp / jnp.sum(near_exp, axis=1, keepdims=True)
     by_cap = jnp.exp(near - cap_lse)
-    row = lax.broadcasted_iota(jnp.int32, (4, CAPS), 0)
-    col = lax.broadcasted_iota(jnp.int32, (4, CAPS), 1)
-    which = jnp.where(row < 2, core, other)
-    mine = (x * ZS + z) * 4 + which * 2 + row % 2
-    eye = jnp.where(mine == col, 1.0, 0.0)
+    eye = jnp.where(chip * 4 + row == col, 1.0, 0.0)
     grad = (by_clip + by_cap - 2.0 * eye) * (LOSS_SCALE * 0.5 / CAPS * LOGIT_SCALE / WORDS * SCALE)
     parts = three_parts(grad)
     spread = jnp.concatenate(
@@ -300,7 +310,9 @@
         ],
         axis=1,
     )
-    of_half = member[pl.ds(pl.multiple_of(core * HALF, HALF), HALF), :]
+    of_half = jnp.concatenate(
+        [member[pl.ds(pl.multiple_of(gx * CHUNK + core * BLOCK, BLOCK), BLOCK), :] for gx in range(XS)], axis=0
+    )
     wide_coef[...] = mm(jnp.concatenate([of_half, of_half, of_half], axis=1), spread, NT)
 
     for copy in core_copies:
@@ -311,7 +323,8 @@
         rows = pl.ds(pl.multiple_of(block * 32, 32), 32)
         part = jnp.zeros((32, DIM), jnp.float32)
         for j in range(4):
-            factor = wide_coef[rows, j * BLOCK : (j + 1) * BLOCK]
+            which = core * 2 + j if j < 2 else other * 2 + j - 2
+            factor = wide_coef[rows, pl.ds(pl.multiple_of(which * BLOCK, BLOCK), BLOCK)]
             factor = jnp.concatenate([factor] * 4, axis=1)
             source = t_own[j, rows, :] if j < 2 else t_recv[j - 2, rows, :].astype(jnp.float32)
             part = part + factor * source
@@ -330,19 +343,29 @@
     sum1[...] = combined(0, 0)
 
     coef = added_parts(mm(parts, member[...], NT), 4)
-    coef_ref[0] = coef[:, :HALF]
-    coef_ref[1] = coef[:, HALF:]
+    for j in range(4):
+        coef_ref[j] = coef[j : j + 1]
     for v in range(2):
         def scaled(p, _, v=v):
             rows = pl.ds(pl.multiple_of(p * 112, 16), 112)
-            for h in range(2):
-                g = gh_ref[v, h, rows, :].astype(jnp.float32) * coef_ref[h, v : v + 1, :]
-                gs_ref[rows, h * HALF : (h + 1) * HALF] = g.astype(jnp.bfloat16)
+            for gx in range(XS):
+                for h in range(2):
+                    lanes = slice(gx * CHUNK + h * BLOCK, gx * CHUNK + (h + 1) * BLOCK)
+                    g = gh_ref[v, h, rows, gx * BLOCK : (gx + 1) * BLOCK].astype(jnp.float32)
+                    gs_ref[rows, lanes] = (g * coef_ref[core * 2 + v, :, lanes]).astype(jnp.bfloat16)
             return 0
 
         lax.fori_loop(0, 7, scaled, 0)
         rows = pl.ds(v * CLIP_ROWS, CLIP_ROWS)
         pg_ref[rows, :] = mm(gs_ref[...], text_perm[...], NN).astype(jnp.bfloat16)
+
+    terms = jnp.sum(cap_lse, axis=1, keepdims=True)
+    for j, block in enumerate(blocks):
+        clip_top = jnp.max(block, axis=1, keepdims=True)
+        clip_lse = clip_top + jnp.log(jnp.sum(jnp.exp(block - clip_top), axis=1, keepdims=True))
+        matched = jnp.sum(jnp.where(row + 4 * j == col, block, 0.0), axis=1, keepdims=True)
+        terms = terms + jnp.sum(clip_lse - 2.0 * matched, axis=0, keepdims=True)
+    loss_ref[...] = terms * (0.5 / CAPS)
 
     for copy in copies1:
         copy.wait()
@@ -353,7 +376,8 @@
         own2[m] = summed[:, m * BLOCK : (m + 1) * BLOCK]
     for j in range(ZS):
         part = jnp.concatenate([own2[m, pl.ds(j, 4, stride=8), :] for m in range(4)], axis=1)
-        snd2[j] = part
+        own3[j] = part
+        snd2[j] = part.astype(jnp.bfloat16)
     copies2 = []
     for i in (4, 3, 5, 2, 6, 1, 7):
         b = lax.rem(z + i, ZS)
@@ -364,11 +388,11 @@
         )
         copy.start()
         copies2.append(copy)
-    result = snd2[z]
+    result = own3[z]
     for copy in copies2:
         copy.wait()
     for i in range(ZS - 1):
-        result = result + rcv2[i]
+        result = result + rcv2[i].astype(jnp.float32)
     tg_ref[...] = result
 
 
@@ -409,22 +433,23 @@
             vmem((8, CLIP_ROWS, CHUNK), f32),
             vmem((2, 2, CLIP_ROWS, HALF), bf16),
             vmem((YS, 2, 2, ROWS), f32),
-            vmem((XS * CS, 2, CAPS), f32),
-            vmem((ZS, 16, CAPS), f32),
+            vmem((CS, 2, CAPS), f32),
+            vmem((CHIP_COUNT, 4, CAPS), f32),
             vmem((2, HALF, DIM), f32),
             vmem((2, HALF, DIM), bf16),
             vmem((2, HALF, DIM), bf16),
-            vmem((2, 4, HALF), f32),
+            vmem((4, 1, ROWS), f32),
             vmem((HALF, 4 * BLOCK), f32),
             vmem((15, 32, DIM), bf16),
             vmem((15, 32, DIM), bf16),
             vmem((32, DIM), f32),
+            vmem((ZS, 4, DIM), bf16),
+            vmem((4, 32, BLOCK), f32),
             vmem((ZS, 4, DIM), f32),
-            vmem((4, 32, BLOCK), f32),
-            vmem((ZS - 1, 4, DIM), f32),
+            vmem((ZS - 1, 4, DIM), bf16),
             vmem((CLIP_ROWS, ROWS), bf16),
-            dma, dma((2,)), dma,
-            dma((3,)), dma((3,)), dma((7,)), dma((7,)), dma((7,)), dma((7,)), dma((2,)), dma((2,)),
+            dma((4,)), dma((2,)), dma,
+            dma((3,)), dma((3,)), dma, dma, dma((31,)), dma((31,)), dma((2,)), dma((2,)),
             dma((15,)), dma((15,)), dma((7,)), dma((7,)),
         ],
         compiler_params=pltpu.CompilerParams(

time: 40.2 us -> 40.4 us (level)
  no operation moved by 1% of the time
where the time goes in v3:
time: 40.4 us; the launch traced here: 40.3 us
  Pallas kernels  39.6 us (98%)
  between operations  0.64 us (2%)
    pallas_call x1, Pallas kernels, fused(): pl.pallas_call(kernel, out_shape=shapes, in_specs=[pl.BlockSpec(memory_sp...  37.8 us
    pallas_call x1, Pallas kernels, fused(): pl.pallas_call(store, out_shape=shapes, in_specs=[pl.BlockSpec(memory_spa...  1.82 us

profile of v3, /device:TPU:1, one launch (start us, length us, event | category | flops | bytes accessed | tf_op | source)
XLA Modules:
  0.0 40.3 jit_solution(4605088945212545692)
XLA Ops:
  0.6 37.8 %shard_map.58 = (f32[1,1]{1,0:T(1,128)}, bf16[1568,512]{1,0:T(8,128)(2,1)S(1)}, f32[4,512]{1,0:T(4,128)S(1)}) custom-call(bf16[1024,512]{1,0:T(8,128)(2,1)} %text_hbm.1, bf16[1568,512]{1,0:T(8,128)(2,1)} %bitcast.7, s32[2,16]{1,0:T(2,128)} %slots_hbm.1), custom_call_target="tpu_custom_call" | custom-call | tf_op jit(solution)/shard_map/pallas_call | solution.py:420
  38.5 1.8 %shard_map.59 = (f32[1,1]{1,0:T(1,128)}, bf16[1568,512]{1,0:T(8,128)(2,1)}, f32[4,512]{1,0:T(4,128)}) custom-call(f32[1,1]{1,0:T(1,128)} %get-tuple-element.9.loss_in, bf16[1568,512]{1,0:T(8,128)(2,1)S(1)} %get-tuple-element.10.pg_in, f32[4,512]{1,0:T(4,128)S(1)} %get-tuple-element.11.tg_in), custom_call_target="tpu_custom_call" | custom-call | tf_op jit(solution)/shard_map/pallas_call | solution.py:459

commit v4 on v3

--- a/solution.py
+++ b/solution.py
@@ -56,8 +56,8 @@
 def kernel(
     text_hbm, patch_hbm, slots_hbm,
     loss_ref, pg_ref, tg_ref,
-    text_in, text_wide, text_perm, patch, slots_ref, bias_ref, member,
-    z_ref, gh_ref, cap_rx, pair_rx, chip_rx,
+    text_in, text_perm, patch, slots_ref, bias_ref, member,
+    z_ref, gh_ref, cap_rx, pair_rx, chip_rx, local,
     t_own, t_send, t_recv, coef_ref, wide_coef,
     snd1, rcv1, sum1, snd2, own2, own3, rcv2, gs_ref,
     text_sem, patch_sem, slots_sem,
@@ -112,21 +112,15 @@
     for peer in peers:
         pl.semaphore_signal(barrier, inc=1, device_id=peer, device_id_type=pl.DeviceIdType.MESH)
 
+    q = lax.broadcasted_iota(jnp.int32, (CHUNK, CHUNK), 0)
+    r = lax.broadcasted_iota(jnp.int32, (CHUNK, CHUNK), 1)
+    source = (q % 8) * 32 + (q // 32) * 4 + (q // 8) % 4
+    order = jnp.where(source == r, 1.0, 0.0).astype(jnp.bfloat16)
+
     def arrange(gx):
         text_copies[gx].wait()
         rows = slice(gx * CHUNK, (gx + 1) * CHUNK)
-        for j in range(4):
-            text_wide[j, rows, :] = text_in[rows, j * BLOCK : (j + 1) * BLOCK].astype(jnp.float32)
-        for h in range(2):
-            for gy in range(4):
-                base = gx * CHUNK + h * BLOCK + gy * 32
-                for j in range(4):
-                    pieces = []
-                    for k in range(4):
-                        start = gx * CHUNK + h * 16 + gy * 4 + k
-                        pieces.append(text_wide[j, pl.ds(start, 8, stride=32), :])
-                    group = jnp.concatenate(pieces, axis=0).astype(jnp.bfloat16)
-                    text_perm[base : base + 32, j * BLOCK : (j + 1) * BLOCK] = group
+        text_perm[rows, :] = mm(order, text_in[rows, :], NN).astype(jnp.bfloat16)
 
     def tiled(value):
         return jnp.broadcast_to(value, (FRAMES, CHUNK))
@@ -161,8 +155,8 @@
         total = jnp.sum(total, axis=0, keepdims=True)
         weighted = jnp.sum(weighted, axis=0, keepdims=True)
         lanes = slice(n * CHUNK, (n + 1) * CHUNK)
-        cap_rx[y, v, 0:1, lanes] = peak + jnp.log(total) * LOG2E
-        cap_rx[y, v, 1:2, lanes] = weighted * SCALE / total
+        local[v, 0:1, lanes] = peak + jnp.log(total) * LOG2E
+        local[v, 1:2, lanes] = weighted * SCALE / total
 
     arrange(0)
     slots_copy.wait()
@@ -175,17 +169,17 @@
         column = jnp.sum(spread, axis=1, keepdims=True)
         bias_ref[v] = jnp.broadcast_to(column, (FRAMES, BLOCK))
 
+    for n in range(1, XS):
+        arrange(n)
     patch_copies[0].wait()
+    patch_copies[1].wait()
     multiply(0)
     for i in range(8):
-        if i < 3:
-            arrange(i + 1)
-        if i == 3:
-            patch_copies[1].wait()
         if i < 7:
             multiply(i + 1)
         statistics(i)
 
+    cap_rx[y] = local[...]
     pl.semaphore_wait(barrier, len(peers))
 
     cap_copies = []
@@ -248,7 +242,6 @@
 
         lax.fori_loop(0, 4, body, 0)
 
-    shaped(0, other)
     pair_copy.wait()
     chip_rx[chip] = jnp.concatenate([pair_rx[0], pair_rx[1]], axis=0)
     chip_copies = []
@@ -263,8 +256,7 @@
 
     core_copies = []
     for v in range(2):
-        if v:
-            shaped(v, other)
+        shaped(v, other)
         clip_patch = patch[v * CLIP_ROWS : (v + 1) * CLIP_ROWS, :]
         t_send[v] = mm(gh_ref[v, other], clip_patch, TN).astype(jnp.bfloat16)
         copy = pltpu.make_async_remote_copy(
@@ -424,7 +416,6 @@
         out_specs=(pl.BlockSpec(memory_space=vmem),) * 3,
         scratch_shapes=[
             vmem((ROWS, DIM), bf16),
-            vmem((4, ROWS, BLOCK), f32),
             vmem((ROWS, DIM), bf16),
             vmem((2 * CLIP_ROWS, DIM), bf16),
             vmem((2, FRAMES), jnp.int32),
@@ -435,6 +426,7 @@
             vmem((YS, 2, 2, ROWS), f32),
             vmem((CS, 2, CAPS), f32),
             vmem((CHIP_COUNT, 4, CAPS), f32),
+            vmem((2, 2, ROWS), f32),
             vmem((2, HALF, DIM), f32),
             vmem((2, HALF, DIM), bf16),
             vmem((2, HALF, DIM), bf16),

time: 40.4 us -> 39.4 us (0.975)
  Pallas kernels: 39.6 us -> 38.6 us
    pallas_call x1, Pallas kernels: 37.8 us -> 36.8 us  [fused(): pl.pallas_call(kernel, out_shape=shapes, in_specs=[pl.BlockSpec(memory_sp...]
where the time goes in v4:
time: 39.4 us; the launch traced here: 39.3 us
  Pallas kernels  38.6 us (98%)
  between operations  0.64 us (2%)
    pallas_call x1, Pallas kernels, fused(): pl.pallas_call(kernel, out_shape=shapes, in_specs=[pl.BlockSpec(memory_sp...  36.8 us
    pallas_call x1, Pallas kernels, fused(): pl.pallas_call(store, out_shape=shapes, in_specs=[pl.BlockSpec(memory_spa...  1.82 us

profile of v4, /device:TPU:1, one launch (start us, length us, event | category | flops | bytes accessed | tf_op | source)
XLA Modules:
  0.0 39.3 jit_solution(12474214377516092523)
XLA Ops:
  0.6 36.8 %shard_map.58 = (f32[1,1]{1,0:T(1,128)}, bf16[1568,512]{1,0:T(8,128)(2,1)S(1)}, f32[4,512]{1,0:T(4,128)S(1)}) custom-call(bf16[1024,512]{1,0:T(8,128)(2,1)} %text_hbm.1, bf16[1568,512]{1,0:T(8,128)(2,1)} %bitcast.7, s32[2,16]{1,0:T(2,128)} %slots_hbm.1), custom_call_target="tpu_custom_call" | custom-call | tf_op jit(solution)/shard_map/pallas_call | solution.py:412
  37.4 1.8 %shard_map.59 = (f32[1,1]{1,0:T(1,128)}, bf16[1568,512]{1,0:T(8,128)(2,1)}, f32[4,512]{1,0:T(4,128)}) custom-call(f32[1,1]{1,0:T(1,128)} %get-tuple-element.9.loss_in, bf16[1568,512]{1,0:T(8,128)(2,1)S(1)} %get-tuple-element.10.pg_in, f32[4,512]{1,0:T(4,128)S(1)} %get-tuple-element.11.tg_in), custom_call_target="tpu_custom_call" | custom-call | tf_op jit(solution)/shard_map/pallas_call | solution.py:451

commit v5 on v4

--- a/solution.py
+++ b/solution.py
@@ -84,12 +84,9 @@
         patch_copies.append(pltpu.make_async_copy(patch_hbm.at[rows], patch.at[rows], patch_sem.at[v]))
         patch_copies[-1].start()
 
-    fetch_text(0)
+    for n in range(XS):
+        fetch_text(n)
     slots_copy.start()
-    fetch_patch(0)
-    for n in range(1, XS):
-        fetch_text(n)
-    fetch_patch(1)
 
     def far_peer(i):
         return (x, lax.rem(z + i, ZS), core, y)
@@ -109,7 +106,10 @@
     peers = [chip_peer(dx, dz) for dx, dz in CHIPS]
     peers += [plane_peer(dx, dy) for dx, dy in PLANE if dy]
     peers.append(twin)
-    for peer in peers:
+    for n, peer in enumerate(peers):
+        if n == 24:
+            fetch_patch(0)
+            fetch_patch(1)
         pl.semaphore_signal(barrier, inc=1, device_id=peer, device_id_type=pl.DeviceIdType.MESH)
 
     q = lax.broadcasted_iota(jnp.int32, (CHUNK, CHUNK), 0)
@@ -199,7 +199,7 @@
     member[...] = jnp.where(caption == c, 1.0, 0.0).astype(jnp.bfloat16)
 
     for copy in cap_copies:
-        copy.wait()
+        copy.wait_recv()
 
     lse, pooled = [], []
     for v in range(2):
@@ -222,27 +222,29 @@
     )
     pair_copy.start()
 
+    for copy in cap_copies:
+        copy.wait_send()
     for v in range(2):
         cap_rx[y, v, 0:1, :] = lse[v]
         cap_rx[y, v, 1:2, :] = 1.0 - pooled[v]
 
     def shaped(v, half):
-        def body(n, _):
+        near = pl.ds(pl.multiple_of(half * BLOCK, BLOCK), BLOCK)
+        for n in range(XS):
             lanes = pl.ds(pl.multiple_of(n * CHUNK + half * BLOCK, BLOCK), BLOCK)
-            near = pl.ds(pl.multiple_of(half * BLOCK, BLOCK), BLOCK)
-            inner = pl.ds(pl.multiple_of(n * BLOCK, BLOCK), BLOCK)
             offset = bias_ref[v] - jnp.broadcast_to(cap_rx[y, v, 0:1, lanes], (FRAMES, BLOCK))
             shift = jnp.broadcast_to(cap_rx[y, v, 1:2, lanes], (FRAMES, BLOCK))
             for p in range(PATCH):
-                s = z_ref[v * 4 + n, p * FRAMES : (p + 1) * FRAMES, near]
+                rows = slice(p * FRAMES, (p + 1) * FRAMES)
+                s = z_ref[v * 4 + n, rows, near]
                 w = jnp.exp2(s * (SCALE * LOG2E) + offset)
                 g = w * (s * SCALE + shift)
-                gh_ref[v, half, p * FRAMES : (p + 1) * FRAMES, inner] = g.astype(jnp.bfloat16)
-            return 0
-
-        lax.fori_loop(0, 4, body, 0)
-
-    pair_copy.wait()
+                gh_ref[v, half, rows, n * BLOCK : (n + 1) * BLOCK] = g.astype(jnp.bfloat16)
+
+    def turned(v, half):
+        return mm(gh_ref[v, half], patch[v * CLIP_ROWS : (v + 1) * CLIP_ROWS, :], TN)
+
+    pair_copy.wait_recv()
     chip_rx[chip] = jnp.concatenate([pair_rx[0], pair_rx[1]], axis=0)
     chip_copies = []
     for slot, (dx, dz) in enumerate(CHIPS):
@@ -254,25 +256,28 @@
         copy.start()
         chip_copies.append(copy)
 
-    core_copies = []
-    for v in range(2):
-        shaped(v, other)
-        clip_patch = patch[v * CLIP_ROWS : (v + 1) * CLIP_ROWS, :]
-        t_send[v] = mm(gh_ref[v, other], clip_patch, TN).astype(jnp.bfloat16)
+    def to_twin(v):
         copy = pltpu.make_async_remote_copy(
             src_ref=t_send.at[v], dst_ref=t_recv.at[v],
             send_sem=core_ss.at[v], recv_sem=core_rs.at[v],
             device_id=twin, device_id_type=pl.DeviceIdType.MESH,
         )
         copy.start()
-        core_copies.append(copy)
-
-    for v in range(2):
-        shaped(v, core)
-        t_own[v] = mm(gh_ref[v, core], patch[v * CLIP_ROWS : (v + 1) * CLIP_ROWS, :], TN)
+        return copy
+
+    shaped(0, other)
+    t_send[0] = turned(0, other).astype(jnp.bfloat16)
+    shaped(1, other)
+    core_copies = [to_twin(0)]
+    t_send[1] = turned(1, other).astype(jnp.bfloat16)
+    shaped(0, core)
+    core_copies.append(to_twin(1))
+    t_own[0] = turned(0, core)
+    shaped(1, core)
+    t_own[1] = turned(1, core)
 
     for copy in chip_copies:
-        copy.wait()
+        copy.wait_recv()
 
     blocks = [chip_rx[j] for j in range(CHIP_COUNT)]
     cap_top = blocks[0]
@@ -308,7 +313,7 @@
     wide_coef[...] = mm(jnp.concatenate([of_half, of_half, of_half], axis=1), spread, NT)
 
     for copy in core_copies:
-        copy.wait()
+        copy.wait_recv()
 
     def combined(dx, dy):
         block = lax.rem(x + dx, XS) * YS + lax.rem(y + dy, YS)
@@ -360,7 +365,7 @@
     loss_ref[...] = terms * (0.5 / CAPS)
 
     for copy in copies1:
-        copy.wait()
+        copy.wait_recv()
     summed = sum1[...]
     for slot in range(len(PLANE)):
         summed = summed + rcv1[slot].astype(jnp.float32)
@@ -381,11 +386,15 @@
         copy.start()
         copies2.append(copy)
     result = own3[z]
+    for copy in [pair_copy] + core_copies + chip_copies + copies1:
+        copy.wait_send()
     for copy in copies2:
-        copy.wait()
+        copy.wait_recv()
     for i in range(ZS - 1):
         result = result + rcv2[i].astype(jnp.float32)
     tg_ref[...] = result
+    for copy in copies2:
+        copy.wait_send()
 
 
 def store(loss_in, pg_in, tg_in, loss_out, pg_out, tg_out, sems):

time: 39.4 us -> 38.7 us (0.982)
  Pallas kernels: 38.6 us -> 37.9 us
    pallas_call x1, Pallas kernels: 36.8 us -> 36.1 us  [fused(): pl.pallas_call(kernel, out_shape=shapes, in_specs=[pl.BlockSpec(memory_sp...]
where the time goes in v5:
time: 38.7 us; the launch traced here: 38.6 us
  Pallas kernels  37.9 us (98%)
  between operations  0.64 us (2%)
    pallas_call x1, Pallas kernels, fused(): pl.pallas_call(kernel, out_shape=shapes, in_specs=[pl.BlockSpec(memory_sp...  36.1 us
    pallas_call x1, Pallas kernels, fused(): pl.pallas_call(store, out_shape=shapes, in_specs=[pl.BlockSpec(memory_spa...  1.82 us

profile of v5, /device:TPU:1, one launch (start us, length us, event | category | flops | bytes accessed | tf_op | source)
XLA Modules:
  0.0 38.6 jit_solution(12196161041988025987)
XLA Ops:
  0.6 36.1 %shard_map.58 = (f32[1,1]{1,0:T(1,128)}, bf16[1568,512]{1,0:T(8,128)(2,1)S(1)}, f32[4,512]{1,0:T(4,128)S(1)}) custom-call(bf16[1024,512]{1,0:T(8,128)(2,1)} %text_hbm.1, bf16[1568,512]{1,0:T(8,128)(2,1)} %bitcast.7, s32[2,16]{1,0:T(2,128)} %slots_hbm.1), custom_call_target="tpu_custom_call" | custom-call | tf_op jit(solution)/shard_map/pallas_call | solution.py:421
  36.8 1.8 %shard_map.59 = (f32[1,1]{1,0:T(1,128)}, bf16[1568,512]{1,0:T(8,128)(2,1)}, f32[4,512]{1,0:T(4,128)}) custom-call(f32[1,1]{1,0:T(1,128)} %get-tuple-element.9.loss_in, bf16[1568,512]{1,0:T(8,128)(2,1)S(1)} %get-tuple-element.10.pg_in, f32[4,512]{1,0:T(4,128)S(1)} %get-tuple-element.11.tg_in), custom_call_target="tpu_custom_call" | custom-call | tf_op jit(solution)/shard_map/pallas_call | solution.py:460

commit v6 on v5

--- a/solution.py
+++ b/solution.py
@@ -364,10 +364,9 @@
         terms = terms + jnp.sum(clip_lse - 2.0 * matched, axis=0, keepdims=True)
     loss_ref[...] = terms * (0.5 / CAPS)
 
-    for copy in copies1:
+    summed = sum1[...]
+    for slot, copy in enumerate(copies1):
         copy.wait_recv()
-    summed = sum1[...]
-    for slot in range(len(PLANE)):
         summed = summed + rcv1[slot].astype(jnp.float32)
     for m in range(4):
         own2[m] = summed[:, m * BLOCK : (m + 1) * BLOCK]
@@ -388,10 +387,9 @@
     result = own3[z]
     for copy in [pair_copy] + core_copies + chip_copies + copies1:
         copy.wait_send()
-    for copy in copies2:
+    for i, copy in zip((4, 3, 5, 2, 6, 1, 7), copies2):
         copy.wait_recv()
-    for i in range(ZS - 1):
-        result = result + rcv2[i].astype(jnp.float32)
+        result = result + rcv2[i - 1].astype(jnp.float32)
     tg_ref[...] = result
     for copy in copies2:
         copy.wait_send()

time: 38.7 us -> 38.6 us (level)
  no operation moved by 1% of the time
where the time goes in v6:
time: 38.6 us; the launch traced here: 38.5 us
  Pallas kernels  37.9 us (98%)
  between operations  0.64 us (2%)
    pallas_call x1, Pallas kernels, fused(): pl.pallas_call(kernel, out_shape=shapes, in_specs=[pl.BlockSpec(memory_sp...  36.1 us
    pallas_call x1, Pallas kernels, fused(): pl.pallas_call(store, out_shape=shapes, in_specs=[pl.BlockSpec(memory_spa...  1.82 us

profile of v6, /device:TPU:1, one launch (start us, length us, event | category | flops | bytes accessed | tf_op | source)
XLA Modules:
  0.0 38.5 jit_solution(1728368617694554871)
XLA Ops:
  0.6 36.1 %shard_map.58 = (f32[1,1]{1,0:T(1,128)}, bf16[1568,512]{1,0:T(8,128)(2,1)S(1)}, f32[4,512]{1,0:T(4,128)S(1)}) custom-call(bf16[1024,512]{1,0:T(8,128)(2,1)} %text_hbm.1, bf16[1568,512]{1,0:T(8,128)(2,1)} %bitcast.7, s32[2,16]{1,0:T(2,128)} %slots_hbm.1), custom_call_target="tpu_custom_call" | custom-call | tf_op jit(solution)/shard_map/pallas_call | solution.py:419
  36.7 1.8 %shard_map.59 = (f32[1,1]{1,0:T(1,128)}, bf16[1568,512]{1,0:T(8,128)(2,1)}, f32[4,512]{1,0:T(4,128)}) custom-call(f32[1,1]{1,0:T(1,128)} %get-tuple-element.9.loss_in, bf16[1568,512]{1,0:T(8,128)(2,1)S(1)} %get-tuple-element.10.pg_in, f32[4,512]{1,0:T(4,128)S(1)} %get-tuple-element.11.tg_in), custom_call_target="tpu_custom_call" | custom-call | tf_op jit(solution)/shard_map/pallas_call | solution.py:458
